TPU v7x, 128 devices: a whole 4x4x4 slice. The times are simulated.
128 devices in a mesh: sky: 16 (over x, z), depth: 8 (over y, core).
Axes of the slice: x: 4, y: 4, z: 4, core: 2. Of those that a mesh axis runs over, the one named last changes fastest.
Arguments:
- positions: float32 [3, 2048, 128], P(None, ('sky', 'depth')), may hold values from 0 to 1
- cell_points: int32 [2048], P(('sky', 'depth')), may hold values from 1 to 128
- target_log: float32 [16], replicated, may hold values from 8 to 20
- export_count: int32 [128, 128], P(('sky', 'depth')), may hold values from 0 to 3, as said below
- export_cell: int32 [128, 128, 3], P(('sky', 'depth')), may hold values from 0 to 15
- import_pair: int32 [128, 128, 3], P(('sky', 'depth')), may hold values from 0 to 15
- import_shift: int32 [3, 128, 128, 3], P(None, ('sky', 'depth')), may hold values from -1 to 1, as said below
Outputs:
- travel: float32 [3, 2048, 128], P(None, ('sky', 'depth'))
Inputs may be any that keep to these rules, and one draw needn't show every extreme that they name: export_count[s, t] counts the slots of export_cell[s, t] that are used; it is zero unless s and t are distinct devices whose sky indices differ by at most one modulo the sky axis's size and whose depth indices differ by at most one; in every draw some device t receives 3 cells from each such neighbour. For neighbouring devices t and s, components 0 and 2 of import_shift[:, t, s, k] are the sky step and the depth step from t's region to s's region (sky taken around the cycle), component 1 varies; all components are zero for devices that are not neighbours.
All inputs are finite; a program needn't handle non-finite values.
Results may differ from a plain program's by a relative error of at most 0.00022.
Values sent between devices are 32-bit elements; how exact they have to be, the bound alone decides.
No kernel may reach another device: no remote copies, remote signals or barrier semaphores. Data moves between devices by JAX's collectives and lax.ppermute only.
A program may use at most 64 MiB of HBM per device.

v0:
```python
import jax
import jax.numpy as jnp
from jax import lax
from jax.sharding import PartitionSpec as P

STEPS = 2
EPS_SQ = 0.0001
INV_WIDTH = 16.0
STEP_SIZE = 0.01
ROW_BLOCK = 8


def from_behind(array, axis, by):
    size = lax.axis_size(axis)
    return lax.ppermute(array, axis, [(i, (i + by) % size) for i in range(size)])


def from_behind_2(value, axis, steps):
    count = lax.axis_size(axis)
    initial, last = (max(0, -steps), min(count, count - steps))
    return lax.ppermute(value, axis, [(source, source + steps) for source in range(initial, last)])


def pair_geometry(left_pos, left_mask, right_pos, right_mask, shifts, centres):
    offsets = left_pos[:, :, :, None] - right_pos[:, :, None, :] - shifts[:, :, None, None]
    radius = jnp.sqrt(jnp.sum(offsets * offsets, axis=0) + EPS_SQ)
    weight = left_mask[:, :, None] * right_mask[:, None, :]
    scaled = (radius[None] - centres[:, None, None, None]) * INV_WIDTH
    kernel = jnp.exp(-0.5 * scaled * scaled)
    return (offsets, radius, weight, scaled, kernel)


def block_counts(left_pos, left_mask, right_pos, right_mask, shifts, centres):
    offsets, radius, weight, scaled, kernel = pair_geometry(
        left_pos, left_mask, right_pos, right_mask, shifts, centres
    )
    return jnp.sum(weight[None] * kernel, axis=(1, 2, 3))


def block_forces(left_pos, left_mask, right_pos, right_mask, shifts, centres, bin_pull):
    offsets, radius, weight, scaled, kernel = pair_geometry(
        left_pos, left_mask, right_pos, right_mask, shifts, centres
    )
    slopes = jnp.sum(bin_pull[:, None, None, None] * scaled * kernel, axis=0) * -INV_WIDTH
    strength = weight * slopes / radius
    pulled = strength[None] * offsets
    return (jnp.sum(pulled, axis=3), -jnp.sum(pulled, axis=2))


def take_block(left_pos, left_mask, right_pos, right_mask, shifts, first_row):
    return (
        lax.dynamic_slice_in_dim(left_pos, first_row, ROW_BLOCK, 1),
        lax.dynamic_slice_in_dim(left_mask, first_row, ROW_BLOCK, 0),
        lax.dynamic_slice_in_dim(right_pos, first_row, ROW_BLOCK, 1),
        lax.dynamic_slice_in_dim(right_mask, first_row, ROW_BLOCK, 0),
        lax.dynamic_slice_in_dim(shifts, first_row, ROW_BLOCK, 1),
    )


def ghost_counts(left_pos, left_mask, right_pos, right_mask, shifts, centres):
    block_total = left_pos.shape[1] // ROW_BLOCK

    def add_block(block_id, running):
        pieces = take_block(
            left_pos, left_mask, right_pos, right_mask, shifts, block_id * ROW_BLOCK
        )
        return running + block_counts(
            pieces[0], pieces[1], pieces[2], pieces[3], pieces[4], centres
        )

    return lax.fori_loop(0, block_total, add_block, jnp.zeros(centres.shape, jnp.float32))


def ghost_forces(left_pos, left_mask, right_pos, right_mask, shifts, centres, bin_pull):
    block_total = left_pos.shape[1] // ROW_BLOCK

    def add_block(block_id, buffers):
        first_row = block_id * ROW_BLOCK
        pieces = take_block(left_pos, left_mask, right_pos, right_mask, shifts, first_row)
        force_left, force_right = block_forces(
            pieces[0], pieces[1], pieces[2], pieces[3], pieces[4], centres, bin_pull
        )
        return (
            lax.dynamic_update_slice_in_dim(buffers[0], force_left, first_row, 1),
            lax.dynamic_update_slice_in_dim(buffers[1], force_right, first_row, 1),
        )

    empty = jnp.zeros(left_pos.shape, jnp.float32)
    return lax.fori_loop(0, block_total, add_block, (empty, empty))


def region_offsets():
    return [
        (across, along)
        for across in (-1, 0, 1)
        for along in (-1, 0, 1)
        if (across, along) != (0, 0)
    ]


def neighbour_table():
    sky_here = lax.axis_index("sky")
    depth_here = lax.axis_index("depth")
    sky_count = lax.axis_size("sky")
    depth_count = lax.axis_size("depth")
    near_ids = []
    near_valid = []
    for across, along in region_offsets():
        depth_there = depth_here + along
        inside = (depth_there >= 0) & (depth_there < depth_count)
        clamped = jnp.clip(depth_there, 0, depth_count - 1)
        near_ids.append((sky_here + across) % sky_count * depth_count + clamped)
        near_valid.append(inside)
    return (jnp.stack(near_ids), jnp.stack(near_valid))


def near_sizes(sizes_near):
    received = [None] * 8
    for index, (across, along) in enumerate(region_offsets()):
        piece = sizes_near[index]
        if across != 0:
            piece = from_behind(piece, "sky", across)
        if along != 0:
            piece = from_behind_2(piece, "depth", along)
        received[7 - index] = piece
    return jnp.stack(received)


def near_cells(cells_near):
    received = [None] * 8
    for index, (across, along) in enumerate(region_offsets()):
        piece = cells_near[:, index]
        if across != 0:
            piece = from_behind(piece, "sky", across)
        if along != 0:
            piece = from_behind_2(piece, "depth", along)
        received[7 - index] = piece
    return jnp.stack(received, axis=1)


def near_forces(forces_near):
    received = [None] * 8
    for index, (across, along) in enumerate(region_offsets()):
        piece = forces_near[:, index]
        if across != 0:
            piece = from_behind(piece, "sky", across)
        if along != 0:
            piece = from_behind_2(piece, "depth", along)
        received[7 - index] = piece
    return jnp.stack(received, axis=1)


def send_sizes(sizes_out, near_ids, near_valid):
    return near_sizes(sizes_out[near_ids] * near_valid[:, None].astype(jnp.int32))


def send_cells(coords, export_row, near_ids):
    peer_count, slot_count = export_row.shape
    outgoing = coords[:, export_row[near_ids].reshape(-1)].reshape(
        3, 8, slot_count, coords.shape[2]
    )
    return near_cells(outgoing)


def send_forces(forces_near):
    return near_forces(forces_near)


def body(positions, cell_points, target_log, export_count, export_cell, import_pair, import_shift):
    cell_count = positions.shape[1]
    points = positions.shape[2]
    slot_count = export_cell.shape[2]
    ghosts = 8 * slot_count
    centres = (jnp.arange(target_log.shape[0], dtype=jnp.float32) + 0.5) / INV_WIDTH
    point_ids = jnp.arange(points, dtype=jnp.int32)
    point_mask = (point_ids[None, :] < cell_points[:, None]).astype(jnp.float32)
    cell_ids = jnp.arange(cell_count, dtype=jnp.int32)
    near_ids, near_valid = neighbour_table()
    live_out = jnp.arange(slot_count, dtype=jnp.int32)[None, :] < export_count[0][:, None]
    sizes_out = jnp.where(live_out, cell_points[export_cell[0]], 0)
    sizes_in = send_sizes(sizes_out, near_ids, near_valid)
    ghost_mask = (point_ids[None, :] < sizes_in.reshape(-1)[:, None]).astype(jnp.float32)
    cells_near = export_cell[0][near_ids].reshape(-1)
    live_near = (live_out[near_ids] & near_valid[:, None]).reshape(-1)
    pair_cells = import_pair[0][near_ids].reshape(-1)
    shifts = import_shift[:, 0][:, near_ids].reshape(3, ghosts).astype(jnp.float32)
    left_mask = point_mask[pair_cells]
    onehot_pair = (pair_cells[:, None] == cell_ids[None, :]).astype(jnp.float32)
    onehot_out = ((cells_near[:, None] == cell_ids[None, :]) & live_near[:, None]).astype(
        jnp.float32
    )
    zero_shift = jnp.zeros((3, cell_count), jnp.float32)
    valid_local = jnp.sum(point_mask)
    coords = positions
    travel = jnp.zeros_like(positions)
    for iteration in range(STEPS):
        ghost_pos = send_cells(coords, export_cell[0], near_ids).reshape(3, ghosts, points)
        left_pos = coords[:, pair_cells]
        self_total = block_counts(coords, point_mask, coords, point_mask, zero_shift, centres)
        ghost_total = ghost_counts(left_pos, left_mask, ghost_pos, ghost_mask, shifts, centres)
        counts = lax.psum(0.5 * self_total + ghost_total, ("sky", "depth"))
        mean_count = jnp.mean(counts)
        bin_pull = (jnp.log(1.0 + counts) - target_log) * mean_count / (1.0 + counts)
        self_grad, unused_right = block_forces(
            coords, point_mask, coords, point_mask, zero_shift, centres, bin_pull
        )
        force_left, force_right = ghost_forces(
            left_pos, left_mask, ghost_pos, ghost_mask, shifts, centres, bin_pull
        )
        returned = send_forces(force_right.reshape(3, 8, slot_count, points)).reshape(
            3, ghosts, points
        )
        gradient = self_grad
        gradient = gradient + jnp.einsum(
            "gc,kgp->kcp", onehot_pair, force_left, precision=lax.Precision.HIGHEST
        )
        gradient = gradient + jnp.einsum(
            "gc,kgp->kcp", onehot_out, returned, precision=lax.Precision.HIGHEST
        )
        power_sum, valid_count = lax.psum(
            (jnp.sum(gradient * gradient), valid_local), ("sky", "depth")
        )
        grad_rms = jnp.sqrt(power_sum / (3.0 * valid_count) + 1e-06)
        move_dir = -gradient / grad_rms
        travel = travel + move_dir
        coords = coords + STEP_SIZE * move_dir
    return travel


def solution(mesh):
    in_specs = (
        P(None, ("sky", "depth"), None),
        P(("sky", "depth")),
        P(),
        P(("sky", "depth"), None),
        P(("sky", "depth"), None, None),
        P(("sky", "depth"), None, None),
        P(None, ("sky", "depth"), None, None),
    )
    out_specs = P(None, ("sky", "depth"), None)
    return jax.shard_map(body, mesh=mesh, in_specs=in_specs, out_specs=out_specs, check_vma=False)
```

profile of v0, /device:TPU:1, one launch (start us, length us, event | category | flops | bytes accessed | tf_op | source)
XLA Modules:
  0.0 525.2 jit_solution(16160007866016866266)
XLA Ops:
  0.9 1.9 fusion.81
  3.0 10.6 %fusion.60 = s32[128,3]{1,0:T(8,128)S(1)} fusion(s32[1,128,3]{2,1,0:T(8,128)S(1)} %copy.87, s32[]{:T(128)} %bitcast.31, s32[]{:T(128)} %bitcast.32, s32[]{:T(128)} %bitcast.33, s32[]{:T(128)} %bitcast.34, s32[]{:T(128)} %bitcast.35, s32[]{:T(128)} %bitcast.37, s32[]{:T(128)} %bitcast.36, s32[]{:T(128)} %bitcast.14, s32[]{:T(128)} %bitcast.16, s32[]{:T(128)} %bitcast.18, ...), kind=kLoop, calls=%fused_computation.175 | loop fusion | flops 13440 | bytes 3648 | tf_op jit(solution)/shard_map/jit(_where)/select_n | solution.py:180
  14.3 2.5 collective-permute-start
  19.7 4.6 collective-permute-start.5
  31.1 5.1 fusion.36
  39.6 4.8 collective-permute-start.7
  47.4 5.0 collective-permute-start.17
  55.5 2.1 collective-permute-start.4
  57.6 2.9 collective-permute-done.4
  60.4 2.0 collective-permute-start.8
  63.4 2.1 collective-permute-start.11
  65.6 2.9 collective-permute-done.11
  70.5 3.6 collective-permute-start.13
  74.9 3.4 collective-permute-start.19
  81.1 3.0 collective-permute-start.21
  84.2 5.6 %collective-permute-start.20 = (f32[3,3,128]{2,1,0:T(4,128)S(1)}, f32[3,3,128]{2,1,0:T(4,128)S(1)}, u32[]{:S(2)}, u32[]{:S(2)}) collective-permute-start(f32[3,3,128]{2,1,0:T(4,128)S(1)} %collective-permute-done.19), channel_id=1, source_target_pairs={{0,1},{1,2},{2,3},{3,4},{4,5},{5,6},{6,7},{8,9},{9,10},{10,11},{11... | collective-permute-start | bytes 13832 | tf_op jit(solution)/shard_map/ppermute | solution.py:21
  91.8 2.9 collective-permute-done.23
  94.8 10.7 %while.70 = (s32[]{:T(128)}, f32[16]{0:T(128)S(1)}, f32[24,128]{1,0:T(8,128)S(1)}, f32[24,128]{1,0:T(8,128)S(1)}, f32[3,24,128]{2,1,0:T(8,128)S(1)}, /*index=5*/...) while((s32[]{:T(128)}, f32[16]{0:T(128)S(1)}, ...), condition=%wide.region_5.6_spmd.clone, body=%wide.region_2.5_spmd.clone.sunk | while | flops 14286903 | bytes 3244889 | solution.py:71
  95.8 2.5 fusion.98
  99.3 2.5 fusion.98
  102.9 2.5 fusion.98
  105.6 62.9 %psum.38 = f32[16]{0:T(128)S(1)} all-reduce(f32[16]{0:T(128)S(1)} %multiply_add_fusion.2), channel_id=1, replica_groups=mesh['sky'=16,'depth'=8] {'sky','depth'}, use_global_device_ids=true, to_apply=%region_6.7 | all-reduce | flops 16 | bytes 128 | tf_op jit(solution)/shard_map/psum | solution.py:201
  169.6 5.4 %fusion.37 = f32[16,128,128]{2,1,0:T(8,128)S(1)} fusion(f32[16]{0:T(128)S(1)} %get-tuple-element.1089, f32[16]{0:T(128)S(1)} %add_multiply_fusion.4, f32[16,128,128]{2,1,0:T(8,128)S(1)} %get-tuple-element.1163), kind=kLoop, calls=%fused_computation.105 | loop fusion | flops 29097984 | bytes 2097280 | tf_op jit(solution)/shard_map/reduce_sum | solution.py:44
  175.4 14.3 %while.68 = (s32[]{:T(128)}, f32[3,24,128]{2,1,0:T(8,128)S(1)}, f32[3,24,128]{2,1,0:T(8,128)S(1)}, f32[24,128]{1,0:T(8,128)S(1)}, f32[24,128]{1,0:T(8,128)S(1)},...) while((s32[]{:T(128)}, f32[3,24,128]{2,1,0:T(8,128)S(1)}, ...), condition=%wide.region_15.16_spmd.clone, body=%wide.region_10.0_spmd.clone.sunk | while | flops 18740276 | bytes 4916107 | solution.py:89
  176.2 2.7 fusion.94
  180.9 2.7 fusion.94
  185.7 2.7 fusion.94
  194.3 3.1 collective-permute-start.29
  197.4 1.9 collective-permute-start.30
  199.4 3.6 collective-permute-start.25
  203.8 4.1 collective-permute-start.31
  210.2 3.7 collective-permute-start.33
  213.9 5.3 %collective-permute-start.32 = (f32[3,3,128]{2,1,0:T(4,128)S(1)}, f32[3,3,128]{2,1,0:T(4,128)S(1)}, u32[]{:S(2)}, u32[]{:S(2)}) collective-permute-start(f32[3,3,128]{2,1,0:T(4,128)S(1)} %collective-permute-done.31), channel_id=1, source_target_pairs={{0,1},{1,2},{2,3},{3,4},{4,5},{5,6},{6,7},{8,9},{9,10},{10,11},{11... | collective-permute-start | bytes 13832 | tf_op jit(solution)/shard_map/ppermute | solution.py:21
  219.3 1.9 collective-permute-start.35
  221.3 2.9 collective-permute-done.35
  225.0 62.3 %all-reduce = (f32[]{:T(128)}, f32[]{:T(128)}) all-reduce(f32[]{:T(128)} %get-tuple-element.1159, f32[]{:T(128)} %fusion.76), channel_id=1, replica_groups=mesh['sky'=16,'depth'=8] {'sky','depth'}, use_global_device_ids=true, to_apply=%region_17.18 | all-reduce | flops 2 | bytes 16 | tf_op jit(solution)/shard_map/psum | solution.py:220
  291.5 4.8 collective-permute-done.36
  296.3 4.4 collective-permute-start.37
  300.8 5.1 fusion.42
  306.6 1.9 collective-permute-start.41
  308.6 2.4 collective-permute-start.42
  311.0 4.8 collective-permute-start.43
  319.3 2.5 collective-permute-start.45
  321.8 4.7 collective-permute-start.44
  328.6 2.9 collective-permute-done.47
  331.5 10.7 %while.71 = (s32[]{:T(128)}, f32[16]{0:T(128)S(1)}, f32[24,128]{1,0:T(8,128)S(1)}, f32[24,128]{1,0:T(8,128)S(1)}, f32[3,24,128]{2,1,0:T(8,128)S(1)}, /*index=5*/...) while((s32[]{:T(128)}, f32[16]{0:T(128)S(1)}, ...), condition=%wide.region_25.26_spmd.clone, body=%wide.region_22.25_spmd.clone.sunk | while | flops 14286903 | bytes 3244889 | solution.py:71
  332.5 2.5 fusion.100
  336.1 2.5 fusion.100
  339.7 2.5 fusion.100
  342.2 62.2 %psum.41 = f32[16]{0:T(128)S(1)} all-reduce(f32[16]{0:T(128)S(1)} %multiply_add_fusion.1), channel_id=1, replica_groups=mesh['sky'=16,'depth'=8] {'sky','depth'}, use_global_device_ids=true, to_apply=%region_26.27 | all-reduce | flops 16 | bytes 128 | tf_op jit(solution)/shard_map/psum | solution.py:201
  405.7 5.4 %fusion.43 = f32[16,128,128]{2,1,0:T(8,128)S(1)} fusion(f32[16]{0:T(128)S(1)} %get-tuple-element.1087, f32[16,128,128]{2,1,0:T(8,128)S(1)} %add_sqrt_fusion.4, f32[16]{0:T(128)S(1)} %add_multiply_fusion.4), kind=kLoop, calls=%fused_computation.111 | loop fusion | flops 29097984 | bytes 2097280 | tf_op jit(solution)/shard_map/reduce_sum | solution.py:44
  411.5 14.3 %while.69 = (s32[]{:T(128)}, f32[3,24,128]{2,1,0:T(8,128)S(1)}, f32[3,24,128]{2,1,0:T(8,128)S(1)}, f32[24,128]{1,0:T(8,128)S(1)}, f32[24,128]{1,0:T(8,128)S(1)},...) while((s32[]{:T(128)}, f32[3,24,128]{2,1,0:T(8,128)S(1)}, ...), condition=%wide.region_35.36_spmd.clone, body=%wide.region_30.0_spmd.clone.sunk | while | flops 18740276 | bytes 4916107 | solution.py:89
  412.3 2.7 fusion.96
  417.0 2.7 fusion.96
  421.8 2.7 fusion.96
  428.7 2.0 collective-permute-start.51
  430.7 3.3 collective-permute-start.53
  434.0 1.9 collective-permute-start.54
  435.9 3.6 collective-permute-start.49
  440.3 3.8 collective-permute-start.55
  446.6 3.7 collective-permute-start.57
  450.2 5.3 %collective-permute-start.56 = (f32[3,3,128]{2,1,0:T(4,128)S(1)}, f32[3,3,128]{2,1,0:T(4,128)S(1)}, u32[]{:S(2)}, u32[]{:S(2)}) collective-permute-start(f32[3,3,128]{2,1,0:T(4,128)S(1)} %collective-permute-done.55), channel_id=1, source_target_pairs={{0,1},{1,2},{2,3},{3,4},{4,5},{5,6},{6,7},{8,9},{9,10},{10,11},{11... | collective-permute-start | bytes 13832 | tf_op jit(solution)/shard_map/ppermute | solution.py:21
  457.6 2.9 collective-permute-done.59
  461.3 62.2 %psum.42 = f32[]{:T(128)} all-reduce(f32[]{:T(128)} %get-tuple-element.1161), channel_id=1, replica_groups=mesh['sky'=16,'depth'=8] {'sky','depth'}, use_global_device_ids=true, to_apply=%region_37.38 | all-reduce | flops 1 | bytes 8 | tf_op jit(solution)/shard_map/psum | solution.py:220
  (337 shorter events, 76.0 us)
Async XLA Ops:
  0.0 26.5 %copy-start = (f32[3,16,128]{2,1,0:T(8,128)S(1)}, f32[3,16,128]{2,1,0:T(8,128)}, u32[]{:S(2)}) copy-start(f32[3,16,128]{2,1,0:T(8,128)} %param.15) | copy-start | bytes 73732
  0.0 27.6 %copy-start.3 = (s32[1,128]{1,0:T(1,128)S(1)}, s32[1,128]{1,0:T(1,128)}, u32[]{:S(2)}) copy-start(s32[1,128]{1,0:T(1,128)} %param.18) | copy-start | bytes 1540
  0.0 28.4 %copy-start.5 = (s32[1,128,3]{1,0,2:T(1,128)S(1)}, s32[1,128,3]{1,0,2:T(1,128)}, u32[]{:S(2)}) copy-start(s32[1,128,3]{1,0,2:T(1,128)} %param.20) | copy-start | bytes 4612
  14.3 23.4 %collective-permute-start = (s32[3]{0:T(128)S(1)}, s32[3]{0:T(128)S(1)}, u32[]{:S(2)}, u32[]{:S(2)}) collective-permute-start(s32[3]{0:T(128)S(1)} %get-tuple-element.1142), channel_id=1, source_target_pairs={{0,8},{8,16},{16,24},{24,32},{32,40},{40,48},{48,56},{56,64},{64,7... | collective-permute-start | bytes 44 | tf_op jit(solution)/shard_map/ppermute | solution.py:15
  16.7 22.9 %collective-permute-start.2 = (s32[3]{0:T(128)S(1)}, s32[3]{0:T(128)S(1)}, u32[]{:S(2)}, u32[]{:S(2)}) collective-permute-start(s32[3]{0:T(128)S(1)} %get-tuple-element.1141), channel_id=1, source_target_pairs={{0,8},{8,16},{16,24},{24,32},{32,40},{40,48},{48,56},{56,64},{64,7... | collective-permute-start | bytes 44 | tf_op jit(solution)/shard_map/ppermute | solution.py:15
  18.4 26.1 %collective-permute-start.3 = (s32[3]{0:T(128)S(1)}, s32[3]{0:T(128)S(1)}, u32[]{:S(2)}, u32[]{:S(2)}) collective-permute-start(s32[3]{0:T(128)S(1)} %get-tuple-element.1140), channel_id=1, source_target_pairs={{0,8},{8,16},{16,24},{24,32},{32,40},{40,48},{48,56},{56,64},{64,7... | collective-permute-start | bytes 44 | tf_op jit(solution)/shard_map/ppermute | solution.py:15
  19.7 24.9 %collective-permute-start.5 = (s32[3]{0:T(128)S(1)}, s32[3]{0:T(128)S(1)}, u32[]{:S(2)}, u32[]{:S(2)}) collective-permute-start(s32[3]{0:T(128)S(1)} %get-tuple-element.1139), channel_id=1, source_target_pairs={{0,1},{1,2},{2,3},{3,4},{4,5},{5,6},{6,7},{8,9},{9,10},{10,11},{11... | collective-permute-start | bytes 44 | tf_op jit(solution)/shard_map/ppermute | solution.py:21
  26.4 44.1 %collective-permute-start.12 = (f32[3,3,128]{2,1,0:T(4,128)S(1)}, f32[3,3,128]{2,1,0:T(4,128)S(1)}, u32[]{:S(2)}, u32[]{:S(2)}) collective-permute-start(f32[3,3,128]{2,1,0:T(4,128)S(1)} %get-tuple-element.1133), channel_id=1, source_target_pairs={{0,8},{8,16},{16,24},{24,32},{32,40},{40,48},{48,56},{56,64},{64,7... | collective-permute-start | bytes 13832 | tf_op jit(solution)/shard_map/ppermute | solution.py:15
  37.7 7.0 %collective-permute-start.6 = (s32[3]{0:T(128)S(1)}, s32[3]{0:T(128)S(1)}, u32[]{:S(2)}, u32[]{:S(2)}) collective-permute-start(s32[3]{0:T(128)S(1)} %get-tuple-element.1138), channel_id=1, source_target_pairs={{1,0},{2,1},{3,2},{4,3},{5,4},{6,5},{7,6},{9,8},{10,9},{11,10},{12... | collective-permute-start | bytes 44 | tf_op jit(solution)/shard_map/ppermute | solution.py:21
  39.6 6.4 %collective-permute-start.7 = (s32[3]{0:T(128)S(1)}, s32[3]{0:T(128)S(1)}, u32[]{:S(2)}, u32[]{:S(2)}) collective-permute-start(s32[3]{0:T(128)S(1)} %get-tuple-element.1137), channel_id=1, source_target_pairs={{0,120},{8,0},{16,8},{24,16},{32,24},{40,32},{48,40},{56,48},{64,5... | collective-permute-start | bytes 44 | tf_op jit(solution)/shard_map/ppermute | solution.py:15
  44.5 2.9 collective-permute-start.9
  44.6 7.9 %collective-permute-start.10 = (s32[3]{0:T(128)S(1)}, s32[3]{0:T(128)S(1)}, u32[]{:S(2)}, u32[]{:S(2)}) collective-permute-start(s32[3]{0:T(128)S(1)} %get-tuple-element.1135), channel_id=1, source_target_pairs={{0,120},{8,0},{16,8},{24,16},{32,24},{40,32},{48,40},{56,48},{64,5... | collective-permute-start | bytes 44 | tf_op jit(solution)/shard_map/ppermute | solution.py:15
  44.7 33.7 %collective-permute-start.14 = (f32[3,3,128]{2,1,0:T(4,128)S(1)}, f32[3,3,128]{2,1,0:T(4,128)S(1)}, u32[]{:S(2)}, u32[]{:S(2)}) collective-permute-start(f32[3,3,128]{2,1,0:T(4,128)S(1)} %get-tuple-element.1132), channel_id=1, source_target_pairs={{0,8},{8,16},{16,24},{24,32},{32,40},{40,48},{48,56},{56,64},{64,7... | collective-permute-start | bytes 13832 | tf_op jit(solution)/shard_map/ppermute | solution.py:15
  46.1 33.1 %collective-permute-start.15 = (f32[3,3,128]{2,1,0:T(4,128)S(1)}, f32[3,3,128]{2,1,0:T(4,128)S(1)}, u32[]{:S(2)}, u32[]{:S(2)}) collective-permute-start(f32[3,3,128]{2,1,0:T(4,128)S(1)} %get-tuple-element.1131), channel_id=1, source_target_pairs={{0,8},{8,16},{16,24},{24,32},{32,40},{40,48},{48,56},{56,64},{64,7... | collective-permute-start | bytes 13832 | tf_op jit(solution)/shard_map/ppermute | solution.py:15
  47.4 44.3 %collective-permute-start.17 = (f32[3,3,128]{2,1,0:T(4,128)S(1)}, f32[3,3,128]{2,1,0:T(4,128)S(1)}, u32[]{:S(2)}, u32[]{:S(2)}) collective-permute-start(f32[3,3,128]{2,1,0:T(4,128)S(1)} %get-tuple-element.1130), channel_id=1, source_target_pairs={{0,1},{1,2},{2,3},{3,4},{4,5},{5,6},{6,7},{8,9},{9,10},{10,11},{11... | collective-permute-start | bytes 13832 | tf_op jit(solution)/shard_map/ppermute | solution.py:21
  52.5 3.0 collective-permute-start.1
  55.5 5.0 collective-permute-start.4
  60.4 3.0 collective-permute-start.8
  63.4 5.0 collective-permute-start.11
  68.5 23.3 %collective-permute-start.18 = (f32[3,3,128]{2,1,0:T(4,128)S(1)}, f32[3,3,128]{2,1,0:T(4,128)S(1)}, u32[]{:S(2)}, u32[]{:S(2)}) collective-permute-start(f32[3,3,128]{2,1,0:T(4,128)S(1)} %get-tuple-element.1129), channel_id=1, source_target_pairs={{1,0},{2,1},{3,2},{4,3},{5,4},{6,5},{7,6},{9,8},{10,9},{11,10},{12... | collective-permute-start | bytes 13832 | tf_op jit(solution)/shard_map/ppermute | solution.py:21
  70.5 4.4 collective-permute-start.13
  74.9 6.2 %collective-permute-start.19 = (f32[3,3,128]{2,1,0:T(4,128)S(1)}, f32[3,3,128]{2,1,0:T(4,128)S(1)}, u32[]{:S(2)}, u32[]{:S(2)}) collective-permute-start(f32[3,3,128]{2,1,0:T(4,128)S(1)} %get-tuple-element.1128), channel_id=1, source_target_pairs={{0,120},{8,0},{16,8},{24,16},{32,24},{40,32},{48,40},{56,48},{64,5... | collective-permute-start | bytes 13832 | tf_op jit(solution)/shard_map/ppermute | solution.py:15
  78.4 5.8 %collective-permute-start.22 = (f32[3,3,128]{2,1,0:T(4,128)S(1)}, f32[3,3,128]{2,1,0:T(4,128)S(1)}, u32[]{:S(2)}, u32[]{:S(2)}) collective-permute-start(f32[3,3,128]{2,1,0:T(4,128)S(1)} %get-tuple-element.1127), channel_id=1, source_target_pairs={{0,120},{8,0},{16,8},{24,16},{32,24},{40,32},{48,40},{56,48},{64,5... | collective-permute-start | bytes 13832 | tf_op jit(solution)/shard_map/ppermute | solution.py:15
  79.2 10.6 %collective-permute-start.16 = (f32[3,3,128]{2,1,0:T(4,128)S(1)}, f32[3,3,128]{2,1,0:T(4,128)S(1)}, u32[]{:S(2)}, u32[]{:S(2)}) collective-permute-start(f32[3,3,128]{2,1,0:T(4,128)S(1)} %collective-permute-done.15), channel_id=1, source_target_pairs={{1,0},{2,1},{3,2},{4,3},{5,4},{6,5},{7,6},{9,8},{10,9},{11,10},{12... | collective-permute-start | bytes 13832 | tf_op jit(solution)/shard_map/ppermute | solution.py:21
  81.1 10.7 %collective-permute-start.21 = (f32[3,3,128]{2,1,0:T(4,128)S(1)}, f32[3,3,128]{2,1,0:T(4,128)S(1)}, u32[]{:S(2)}, u32[]{:S(2)}) collective-permute-start(f32[3,3,128]{2,1,0:T(4,128)S(1)} %get-tuple-element.1134), channel_id=1, source_target_pairs={{0,120},{8,0},{16,8},{24,16},{32,24},{40,32},{48,40},{56,48},{64,5... | collective-permute-start | bytes 13832 | tf_op jit(solution)/shard_map/ppermute | solution.py:15
  84.2 7.6 %collective-permute-start.20 = (f32[3,3,128]{2,1,0:T(4,128)S(1)}, f32[3,3,128]{2,1,0:T(4,128)S(1)}, u32[]{:S(2)}, u32[]{:S(2)}) collective-permute-start(f32[3,3,128]{2,1,0:T(4,128)S(1)} %collective-permute-done.19), channel_id=1, source_target_pairs={{0,1},{1,2},{2,3},{3,4},{4,5},{5,6},{6,7},{8,9},{9,10},{10,11},{11... | collective-permute-start | bytes 13832 | tf_op jit(solution)/shard_map/ppermute | solution.py:21
  89.8 4.9 collective-permute-start.23
  94.8 74.8 %copy-start.4 = (f32[16]{0:T(128)S(1)}, f32[16]{0:T(128)}, u32[]{:S(2)}) copy-start(f32[16]{0:T(128)} %param.17) | copy-start | bytes 196
  189.7 9.6 %collective-permute-start.24 = (f32[3,3,128]{2,1,0:T(4,128)S(1)}, f32[3,3,128]{2,1,0:T(4,128)S(1)}, u32[]{:S(2)}, u32[]{:S(2)}) collective-permute-start(f32[3,3,128]{2,1,0:T(4,128)S(1)} %get-tuple-element.1125), channel_id=1, source_target_pairs={{0,8},{8,16},{16,24},{24,32},{32,40},{40,48},{48,56},{56,64},{64,7... | collective-permute-start | bytes 13832 | tf_op jit(solution)/shard_map/ppermute | solution.py:15
  192.2 15.6 %collective-permute-start.26 = (f32[3,3,128]{2,1,0:T(4,128)S(1)}, f32[3,3,128]{2,1,0:T(4,128)S(1)}, u32[]{:S(2)}, u32[]{:S(2)}) collective-permute-start(f32[3,3,128]{2,1,0:T(4,128)S(1)} %get-tuple-element.1124), channel_id=1, source_target_pairs={{0,8},{8,16},{16,24},{24,32},{32,40},{40,48},{48,56},{56,64},{64,7... | collective-permute-start | bytes 13832 | tf_op jit(solution)/shard_map/ppermute | solution.py:15
  192.6 15.6 %collective-permute-start.27 = (f32[3,3,128]{2,1,0:T(4,128)S(1)}, f32[3,3,128]{2,1,0:T(4,128)S(1)}, u32[]{:S(2)}, u32[]{:S(2)}) collective-permute-start(f32[3,3,128]{2,1,0:T(4,128)S(1)} %get-tuple-element.1123), channel_id=1, source_target_pairs={{0,8},{8,16},{16,24},{24,32},{32,40},{40,48},{48,56},{56,64},{64,7... | collective-permute-start | bytes 13832 | tf_op jit(solution)/shard_map/ppermute | solution.py:15
  194.3 26.9 %collective-permute-start.29 = (f32[3,3,128]{2,1,0:T(4,128)S(1)}, f32[3,3,128]{2,1,0:T(4,128)S(1)}, u32[]{:S(2)}, u32[]{:S(2)}) collective-permute-start(f32[3,3,128]{2,1,0:T(4,128)S(1)} %get-tuple-element.1122), channel_id=1, source_target_pairs={{0,1},{1,2},{2,3},{3,4},{4,5},{5,6},{6,7},{8,9},{9,10},{10,11},{11... | collective-permute-start | bytes 13832 | tf_op jit(solution)/shard_map/ppermute | solution.py:21
  197.4 23.8 %collective-permute-start.30 = (f32[3,3,128]{2,1,0:T(4,128)S(1)}, f32[3,3,128]{2,1,0:T(4,128)S(1)}, u32[]{:S(2)}, u32[]{:S(2)}) collective-permute-start(f32[3,3,128]{2,1,0:T(4,128)S(1)} %get-tuple-element.1121), channel_id=1, source_target_pairs={{1,0},{2,1},{3,2},{4,3},{5,4},{6,5},{7,6},{9,8},{10,9},{11,10},{12... | collective-permute-start | bytes 13832 | tf_op jit(solution)/shard_map/ppermute | solution.py:21
  199.4 4.4 collective-permute-start.25
  203.8 6.4 %collective-permute-start.31 = (f32[3,3,128]{2,1,0:T(4,128)S(1)}, f32[3,3,128]{2,1,0:T(4,128)S(1)}, u32[]{:S(2)}, u32[]{:S(2)}) collective-permute-start(f32[3,3,128]{2,1,0:T(4,128)S(1)} %get-tuple-element.1120), channel_id=1, source_target_pairs={{0,120},{8,0},{16,8},{24,16},{32,24},{40,32},{48,40},{56,48},{64,5... | collective-permute-start | bytes 13832 | tf_op jit(solution)/shard_map/ppermute | solution.py:15
  207.8 6.1 %collective-permute-start.34 = (f32[3,3,128]{2,1,0:T(4,128)S(1)}, f32[3,3,128]{2,1,0:T(4,128)S(1)}, u32[]{:S(2)}, u32[]{:S(2)}) collective-permute-start(f32[3,3,128]{2,1,0:T(4,128)S(1)} %get-tuple-element.1119), channel_id=1, source_target_pairs={{0,120},{8,0},{16,8},{24,16},{32,24},{40,32},{48,40},{56,48},{64,5... | collective-permute-start | bytes 13832 | tf_op jit(solution)/shard_map/ppermute | solution.py:15
  208.2 11.0 %collective-permute-start.28 = (f32[3,3,128]{2,1,0:T(4,128)S(1)}, f32[3,3,128]{2,1,0:T(4,128)S(1)}, u32[]{:S(2)}, u32[]{:S(2)}) collective-permute-start(f32[3,3,128]{2,1,0:T(4,128)S(1)} %collective-permute-done.27), channel_id=1, source_target_pairs={{1,0},{2,1},{3,2},{4,3},{5,4},{6,5},{7,6},{9,8},{10,9},{11,10},{12... | collective-permute-start | bytes 13832 | tf_op jit(solution)/shard_map/ppermute | solution.py:21
  210.2 11.1 %collective-permute-start.33 = (f32[3,3,128]{2,1,0:T(4,128)S(1)}, f32[3,3,128]{2,1,0:T(4,128)S(1)}, u32[]{:S(2)}, u32[]{:S(2)}) collective-permute-start(f32[3,3,128]{2,1,0:T(4,128)S(1)} %get-tuple-element.1126), channel_id=1, source_target_pairs={{0,120},{8,0},{16,8},{24,16},{32,24},{40,32},{48,40},{56,48},{64,5... | collective-permute-start | bytes 13832 | tf_op jit(solution)/shard_map/ppermute | solution.py:15
  213.9 7.4 %collective-permute-start.32 = (f32[3,3,128]{2,1,0:T(4,128)S(1)}, f32[3,3,128]{2,1,0:T(4,128)S(1)}, u32[]{:S(2)}, u32[]{:S(2)}) collective-permute-start(f32[3,3,128]{2,1,0:T(4,128)S(1)} %collective-permute-done.31), channel_id=1, source_target_pairs={{0,1},{1,2},{2,3},{3,4},{4,5},{5,6},{6,7},{8,9},{9,10},{10,11},{11... | collective-permute-start | bytes 13832 | tf_op jit(solution)/shard_map/ppermute | solution.py:21
  219.3 4.9 collective-permute-start.35
  290.2 6.1 %collective-permute-start.36 = (f32[3,3,128]{2,1,0:T(4,128)S(1)}, f32[3,3,128]{2,1,0:T(4,128)S(1)}, u32[]{:S(2)}, u32[]{:S(2)}) collective-permute-start(f32[3,3,128]{2,1,0:T(4,128)S(1)} %bitcast.335), channel_id=1, source_target_pairs={{0,8},{8,16},{16,24},{24,32},{32,40},{40,48},{48,56},{56,64},{64,7... | collective-permute-start | bytes 13832 | tf_op jit(solution)/shard_map/ppermute | solution.py:15
  296.3 14.7 %collective-permute-start.37 = (f32[3,3,128]{2,1,0:T(4,128)S(1)}, f32[3,3,128]{2,1,0:T(4,128)S(1)}, u32[]{:S(2)}, u32[]{:S(2)}) collective-permute-start(f32[3,3,128]{2,1,0:T(4,128)S(1)} %collective-permute-done.36), channel_id=1, source_target_pairs={{0,1},{1,2},{2,3},{3,4},{4,5},{5,6},{6,7},{8,9},{9,10},{10,11},{11... | collective-permute-start | bytes 13832 | tf_op jit(solution)/shard_map/ppermute | solution.py:21
  306.5 9.4 %collective-permute-start.38 = (f32[3,3,128]{2,1,0:T(4,128)S(1)}, f32[3,3,128]{2,1,0:T(4,128)S(1)}, u32[]{:S(2)}, u32[]{:S(2)}) collective-permute-start(f32[3,3,128]{2,1,0:T(4,128)S(1)} %bitcast.332), channel_id=1, source_target_pairs={{0,8},{8,16},{16,24},{24,32},{32,40},{40,48},{48,56},{56,64},{64,7... | collective-permute-start | bytes 13832 | tf_op jit(solution)/shard_map/ppermute | solution.py:15
  306.6 10.8 %collective-permute-start.39 = (f32[3,3,128]{2,1,0:T(4,128)S(1)}, f32[3,3,128]{2,1,0:T(4,128)S(1)}, u32[]{:S(2)}, u32[]{:S(2)}) collective-permute-start(f32[3,3,128]{2,1,0:T(4,128)S(1)} %bitcast.331), channel_id=1, source_target_pairs={{0,8},{8,16},{16,24},{24,32},{32,40},{40,48},{48,56},{56,64},{64,7... | collective-permute-start | bytes 13832 | tf_op jit(solution)/shard_map/ppermute | solution.py:15
  306.6 21.8 %collective-permute-start.41 = (f32[3,3,128]{2,1,0:T(4,128)S(1)}, f32[3,3,128]{2,1,0:T(4,128)S(1)}, u32[]{:S(2)}, u32[]{:S(2)}) collective-permute-start(f32[3,3,128]{2,1,0:T(4,128)S(1)} %bitcast.330), channel_id=1, source_target_pairs={{0,1},{1,2},{2,3},{3,4},{4,5},{5,6},{6,7},{8,9},{9,10},{10,11},{11... | collective-permute-start | bytes 13832 | tf_op jit(solution)/shard_map/ppermute | solution.py:21
  308.6 19.9 %collective-permute-start.42 = (f32[3,3,128]{2,1,0:T(4,128)S(1)}, f32[3,3,128]{2,1,0:T(4,128)S(1)}, u32[]{:S(2)}, u32[]{:S(2)}) collective-permute-start(f32[3,3,128]{2,1,0:T(4,128)S(1)} %bitcast.329), channel_id=1, source_target_pairs={{1,0},{2,1},{3,2},{4,3},{5,4},{6,5},{7,6},{9,8},{10,9},{11,10},{12... | collective-permute-start | bytes 13832 | tf_op jit(solution)/shard_map/ppermute | solution.py:21
  311.0 8.2 %collective-permute-start.43 = (f32[3,3,128]{2,1,0:T(4,128)S(1)}, f32[3,3,128]{2,1,0:T(4,128)S(1)}, u32[]{:S(2)}, u32[]{:S(2)}) collective-permute-start(f32[3,3,128]{2,1,0:T(4,128)S(1)} %bitcast.334), channel_id=1, source_target_pairs={{0,120},{8,0},{16,8},{24,16},{32,24},{40,32},{48,40},{56,48},{64,5... | collective-permute-start | bytes 13832 | tf_op jit(solution)/shard_map/ppermute | solution.py:15
  315.9 5.9 %collective-permute-start.46 = (f32[3,3,128]{2,1,0:T(4,128)S(1)}, f32[3,3,128]{2,1,0:T(4,128)S(1)}, u32[]{:S(2)}, u32[]{:S(2)}) collective-permute-start(f32[3,3,128]{2,1,0:T(4,128)S(1)} %bitcast.333), channel_id=1, source_target_pairs={{0,120},{8,0},{16,8},{24,16},{32,24},{40,32},{48,40},{56,48},{64,5... | collective-permute-start | bytes 13832 | tf_op jit(solution)/shard_map/ppermute | solution.py:15
  317.3 9.2 %collective-permute-start.40 = (f32[3,3,128]{2,1,0:T(4,128)S(1)}, f32[3,3,128]{2,1,0:T(4,128)S(1)}, u32[]{:S(2)}, u32[]{:S(2)}) collective-permute-start(f32[3,3,128]{2,1,0:T(4,128)S(1)} %collective-permute-done.39), channel_id=1, source_target_pairs={{1,0},{2,1},{3,2},{4,3},{5,4},{6,5},{7,6},{9,8},{10,9},{11,10},{12... | collective-permute-start | bytes 13832 | tf_op jit(solution)/shard_map/ppermute | solution.py:21
  319.3 9.3 %collective-permute-start.45 = (f32[3,3,128]{2,1,0:T(4,128)S(1)}, f32[3,3,128]{2,1,0:T(4,128)S(1)}, u32[]{:S(2)}, u32[]{:S(2)}) collective-permute-start(f32[3,3,128]{2,1,0:T(4,128)S(1)} %bitcast.328), channel_id=1, source_target_pairs={{0,120},{8,0},{16,8},{24,16},{32,24},{40,32},{48,40},{56,48},{64,5... | collective-permute-start | bytes 13832 | tf_op jit(solution)/shard_map/ppermute | solution.py:15
  321.8 6.7 %collective-permute-start.44 = (f32[3,3,128]{2,1,0:T(4,128)S(1)}, f32[3,3,128]{2,1,0:T(4,128)S(1)}, u32[]{:S(2)}, u32[]{:S(2)}) collective-permute-start(f32[3,3,128]{2,1,0:T(4,128)S(1)} %collective-permute-done.43), channel_id=1, source_target_pairs={{0,1},{1,2},{2,3},{3,4},{4,5},{5,6},{6,7},{8,9},{9,10},{10,11},{11... | collective-permute-start | bytes 13832 | tf_op jit(solution)/shard_map/ppermute | solution.py:21
  326.5 4.9 collective-permute-start.47
  425.8 10.1 %collective-permute-start.48 = (f32[3,3,128]{2,1,0:T(4,128)S(1)}, f32[3,3,128]{2,1,0:T(4,128)S(1)}, u32[]{:S(2)}, u32[]{:S(2)}) collective-permute-start(f32[3,3,128]{2,1,0:T(4,128)S(1)} %get-tuple-element.1109), channel_id=1, source_target_pairs={{0,8},{8,16},{16,24},{24,32},{32,40},{40,48},{48,56},{56,64},{64,7... | collective-permute-start | bytes 13832 | tf_op jit(solution)/shard_map/ppermute | solution.py:15
  428.5 15.6 %collective-permute-start.50 = (f32[3,3,128]{2,1,0:T(4,128)S(1)}, f32[3,3,128]{2,1,0:T(4,128)S(1)}, u32[]{:S(2)}, u32[]{:S(2)}) collective-permute-start(f32[3,3,128]{2,1,0:T(4,128)S(1)} %get-tuple-element.1108), channel_id=1, source_target_pairs={{0,8},{8,16},{16,24},{24,32},{32,40},{40,48},{48,56},{56,64},{64,7... | collective-permute-start | bytes 13832 | tf_op jit(solution)/shard_map/ppermute | solution.py:15
  428.7 15.9 %collective-permute-start.51 = (f32[3,3,128]{2,1,0:T(4,128)S(1)}, f32[3,3,128]{2,1,0:T(4,128)S(1)}, u32[]{:S(2)}, u32[]{:S(2)}) collective-permute-start(f32[3,3,128]{2,1,0:T(4,128)S(1)} %get-tuple-element.1107), channel_id=1, source_target_pairs={{0,8},{8,16},{16,24},{24,32},{32,40},{40,48},{48,56},{56,64},{64,7... | collective-permute-start | bytes 13832 | tf_op jit(solution)/shard_map/ppermute | solution.py:15
  430.7 26.9 %collective-permute-start.53 = (f32[3,3,128]{2,1,0:T(4,128)S(1)}, f32[3,3,128]{2,1,0:T(4,128)S(1)}, u32[]{:S(2)}, u32[]{:S(2)}) collective-permute-start(f32[3,3,128]{2,1,0:T(4,128)S(1)} %get-tuple-element.1106), channel_id=1, source_target_pairs={{0,1},{1,2},{2,3},{3,4},{4,5},{5,6},{6,7},{8,9},{9,10},{10,11},{11... | collective-permute-start | bytes 13832 | tf_op jit(solution)/shard_map/ppermute | solution.py:21
  434.0 23.5 %collective-permute-start.54 = (f32[3,3,128]{2,1,0:T(4,128)S(1)}, f32[3,3,128]{2,1,0:T(4,128)S(1)}, u32[]{:S(2)}, u32[]{:S(2)}) collective-permute-start(f32[3,3,128]{2,1,0:T(4,128)S(1)} %get-tuple-element.1105), channel_id=1, source_target_pairs={{1,0},{2,1},{3,2},{4,3},{5,4},{6,5},{7,6},{9,8},{10,9},{11,10},{12... | collective-permute-start | bytes 13832 | tf_op jit(solution)/shard_map/ppermute | solution.py:21
  435.9 4.4 collective-permute-start.49
  440.3 6.2 %collective-permute-start.55 = (f32[3,3,128]{2,1,0:T(4,128)S(1)}, f32[3,3,128]{2,1,0:T(4,128)S(1)}, u32[]{:S(2)}, u32[]{:S(2)}) collective-permute-start(f32[3,3,128]{2,1,0:T(4,128)S(1)} %get-tuple-element.1104), channel_id=1, source_target_pairs={{0,120},{8,0},{16,8},{24,16},{32,24},{40,32},{48,40},{56,48},{64,5... | collective-permute-start | bytes 13832 | tf_op jit(solution)/shard_map/ppermute | solution.py:15
  444.1 6.1 %collective-permute-start.58 = (f32[3,3,128]{2,1,0:T(4,128)S(1)}, f32[3,3,128]{2,1,0:T(4,128)S(1)}, u32[]{:S(2)}, u32[]{:S(2)}) collective-permute-start(f32[3,3,128]{2,1,0:T(4,128)S(1)} %get-tuple-element.1103), channel_id=1, source_target_pairs={{0,120},{8,0},{16,8},{24,16},{32,24},{40,32},{48,40},{56,48},{64,5... | collective-permute-start | bytes 13832 | tf_op jit(solution)/shard_map/ppermute | solution.py:15
  444.6 10.9 %collective-permute-start.52 = (f32[3,3,128]{2,1,0:T(4,128)S(1)}, f32[3,3,128]{2,1,0:T(4,128)S(1)}, u32[]{:S(2)}, u32[]{:S(2)}) collective-permute-start(f32[3,3,128]{2,1,0:T(4,128)S(1)} %collective-permute-done.51), channel_id=1, source_target_pairs={{1,0},{2,1},{3,2},{4,3},{5,4},{6,5},{7,6},{9,8},{10,9},{11,10},{12... | collective-permute-start | bytes 13832 | tf_op jit(solution)/shard_map/ppermute | solution.py:21
  446.6 11.0 %collective-permute-start.57 = (f32[3,3,128]{2,1,0:T(4,128)S(1)}, f32[3,3,128]{2,1,0:T(4,128)S(1)}, u32[]{:S(2)}, u32[]{:S(2)}) collective-permute-start(f32[3,3,128]{2,1,0:T(4,128)S(1)} %get-tuple-element.1110), channel_id=1, source_target_pairs={{0,120},{8,0},{16,8},{24,16},{32,24},{40,32},{48,40},{56,48},{64,5... | collective-permute-start | bytes 13832 | tf_op jit(solution)/shard_map/ppermute | solution.py:15
  450.2 7.3 %collective-permute-start.56 = (f32[3,3,128]{2,1,0:T(4,128)S(1)}, f32[3,3,128]{2,1,0:T(4,128)S(1)}, u32[]{:S(2)}, u32[]{:S(2)}) collective-permute-start(f32[3,3,128]{2,1,0:T(4,128)S(1)} %collective-permute-done.55), channel_id=1, source_target_pairs={{0,1},{1,2},{2,3},{3,4},{4,5},{5,6},{6,7},{8,9},{9,10},{10,11},{11... | collective-permute-start | bytes 13832 | tf_op jit(solution)/shard_map/ppermute | solution.py:21
  455.6 4.9 collective-permute-start.59
  (2 other events, 52.8 us)
where the time goes:
time: 535 us; the launch traced here: 525 us
  blocking collectives  250 us (47%)
  starting transfers between devices  140 us (26%)
  other arithmetic  89.7 us (17%)
  waiting for transfers between devices  26.4 us (5%)
  local copies, waits for them, and re-layouts  12.1 us (2%)
    psum x2, blocking collectives, body(): counts = lax.psum(0.5 * self_total + ghost_total, ('sky', 'depth'))  125 us
    psum x2, blocking collectives, body(): lax.psum((jnp.sum(gradient * gradient), valid_local), ('sky', 'depth'))  124 us
    ppermute x30, starting transfers between devices, from_behind_2(): lax.ppermute(value, axis, [(source, source + steps) for source in range(i...  87.8 us
    ppermute x30, starting transfers between devices, from_behind(): lax.ppermute(array, axis, [(i, (i + by) % size) for i in range(size)])  52.4 us
    reduce_sum x8, other arithmetic, block_forces(): jnp.sum(bin_pull[:, None, None, None] * scaled * kernel, axis=0)  26.9 us
    reduce_sum x8, other arithmetic, block_counts(): return jnp.sum(weight[None] * kernel, axis=(1, 2, 3))  25.4 us
    ppermute x30, waiting for transfers between devices, from_behind_2(): lax.ppermute(value, axis, [(source, source + steps) for source in range(i...  21.5 us
  transfers between devices with their start and end apart: 60, of which 12 were waited for; matrix products, arithmetic and copies ran while one was open for 4% of the time, Pallas kernels for 0%

commit v1 on v0

--- a/solution.py
+++ b/solution.py
@@ -198,7 +198,8 @@
         left_pos = coords[:, pair_cells]
         self_total = block_counts(coords, point_mask, coords, point_mask, zero_shift, centres)
         ghost_total = ghost_counts(left_pos, left_mask, ghost_pos, ghost_mask, shifts, centres)
-        counts = lax.psum(0.5 * self_total + ghost_total, ("sky", "depth"))
+        half = lax.psum(0.5 * self_total + ghost_total, "sky")
+        counts = lax.psum(half, "depth")
         mean_count = jnp.mean(counts)
         bin_pull = (jnp.log(1.0 + counts) - target_log) * mean_count / (1.0 + counts)
         self_grad, unused_right = block_forces(

time: 535 us -> 500 us (0.935)
  blocking collectives: 250 us -> 221 us
    psum x2 -> x4, blocking collectives: 125 us -> 95.8 us  [the longest x2 59.5 us: body(): half = lax.psum(0.5 * self_total + ghost_total, 'sky')]
  transfers between devices with their start and end apart: 60 -> 60, of which waited for: 12 -> 12; matrix products, arithmetic and copies ran while one was open for 4% -> 5% of each run, Pallas kernels for 0% -> 0%
where the time goes in v1:
time: 500 us; the launch traced here: 491 us
  blocking collectives  221 us (44%)
  starting transfers between devices  135 us (27%)
  other arithmetic  89.9 us (18%)
  waiting for transfers between devices  26.5 us (5%)
  local copies, waits for them, and re-layouts  12.1 us (2%)
    psum x2, blocking collectives, body(): lax.psum((jnp.sum(gradient * gradient), valid_local), ('sky', 'depth'))  125 us
    ppermute x30, starting transfers between devices, from_behind_2(): lax.ppermute(value, axis, [(source, source + steps) for source in range(i...  85.7 us
    psum x2, blocking collectives, body(): half = lax.psum(0.5 * self_total + ghost_total, 'sky')  59.5 us
    ppermute x30, starting transfers between devices, from_behind(): lax.ppermute(array, axis, [(i, (i + by) % size) for i in range(size)])  48.9 us
    psum x2, blocking collectives, body(): counts = lax.psum(half, 'depth')  36.4 us
    reduce_sum x8, other arithmetic, block_forces(): jnp.sum(bin_pull[:, None, None, None] * scaled * kernel, axis=0)  26.9 us
    reduce_sum x8, other arithmetic, block_counts(): return jnp.sum(weight[None] * kernel, axis=(1, 2, 3))  25.4 us
    ppermute x30, waiting for transfers between devices, from_behind_2(): lax.ppermute(value, axis, [(source, source + steps) for source in range(i...  21.5 us
  transfers between devices with their start and end apart: 60, of which 12 were waited for; matrix products, arithmetic and copies ran while one was open for 5% of the time, Pallas kernels for 0%

profile of v1, /device:TPU:1, one launch (start us, length us, event | category | flops | bytes accessed | tf_op | source)
XLA Modules:
  0.0 491.2 jit_solution(8858545971122071518)
XLA Ops:
  0.9 1.9 fusion.81
  3.0 10.7 %fusion.60 = s32[128,3]{1,0:T(8,128)S(1)} fusion(s32[1,128,3]{2,1,0:T(8,128)S(1)} %copy.87, s32[]{:T(128)} %bitcast.31, s32[]{:T(128)} %bitcast.32, s32[]{:T(128)} %bitcast.33, s32[]{:T(128)} %bitcast.34, s32[]{:T(128)} %bitcast.35, s32[]{:T(128)} %bitcast.37, s32[]{:T(128)} %bitcast.36, s32[]{:T(128)} %bitcast.14, s32[]{:T(128)} %bitcast.16, s32[]{:T(128)} %bitcast.18, ...), kind=kLoop, calls=%fused_computation.175 | loop fusion | flops 13440 | bytes 3648 | tf_op jit(solution)/shard_map/jit(_where)/select_n | solution.py:180
  14.3 2.5 collective-permute-start
  19.8 4.6 collective-permute-start.5
  31.3 5.1 %fusion.36 = f32[16]{0:T(128)S(1)} fusion(f32[16,128,128]{2,1,0:T(8,128)S(1)} %get-tuple-element.1164, f32[16]{0:T(128)S(1)} %add_multiply_fusion.4, f32[16,128,128]{2,1,0:T(8,128)S(1)} %get-tuple-element.1163), kind=kLoop, calls=%fused_computation.104 | loop fusion | flops 25165808 | bytes 2097280 | tf_op jit(solution)/shard_map/reduce_sum | solution.py:37
  37.8 1.9 collective-permute-start.6
  39.8 4.8 collective-permute-start.7
  47.5 5.0 %collective-permute-start.17 = (f32[3,3,128]{2,1,0:T(4,128)S(1)}, f32[3,3,128]{2,1,0:T(4,128)S(1)}, u32[]{:S(2)}, u32[]{:S(2)}) collective-permute-start(f32[3,3,128]{2,1,0:T(4,128)S(1)} %get-tuple-element.1130), channel_id=1, source_target_pairs={{0,1},{1,2},{2,3},{3,4},{4,5},{5,6},{6,7},{8,9},{9,10},{10,11},{11... | collective-permute-start | bytes 13832 | tf_op jit(solution)/shard_map/ppermute | solution.py:21
  52.6 1.9 collective-permute-start.1
  55.6 2.1 collective-permute-start.4
  57.7 2.9 collective-permute-done.4
  60.6 2.0 collective-permute-start.8
  63.6 2.1 collective-permute-start.11
  65.7 2.9 collective-permute-done.11
  70.6 3.6 collective-permute-start.13
  75.0 3.4 collective-permute-start.19
  81.3 3.0 collective-permute-start.21
  84.3 5.6 %collective-permute-start.20 = (f32[3,3,128]{2,1,0:T(4,128)S(1)}, f32[3,3,128]{2,1,0:T(4,128)S(1)}, u32[]{:S(2)}, u32[]{:S(2)}) collective-permute-start(f32[3,3,128]{2,1,0:T(4,128)S(1)} %collective-permute-done.19), channel_id=1, source_target_pairs={{0,1},{1,2},{2,3},{3,4},{4,5},{5,6},{6,7},{8,9},{9,10},{10,11},{11... | collective-permute-start | bytes 13832 | tf_op jit(solution)/shard_map/ppermute | solution.py:21
  92.0 2.9 collective-permute-done.23
  94.9 10.7 %while.70 = (s32[]{:T(128)}, f32[16]{0:T(128)S(1)}, f32[24,128]{1,0:T(8,128)S(1)}, f32[24,128]{1,0:T(8,128)S(1)}, f32[3,24,128]{2,1,0:T(8,128)S(1)}, /*index=5*/...) while((s32[]{:T(128)}, f32[16]{0:T(128)S(1)}, ...), condition=%wide.region_5.6_spmd.clone, body=%wide.region_2.5_spmd.clone.sunk | while | flops 14286903 | bytes 3244889 | solution.py:71
  95.9 2.5 fusion.98
  99.5 2.5 fusion.98
  103.0 2.5 fusion.98
  105.7 29.3 %psum.52 = f32[16]{0:T(128)S(1)} all-reduce(f32[16]{0:T(128)S(1)} %multiply_add_fusion.2), channel_id=1, replica_groups=mesh['sky'=16,'depth'=8] {'sky'}, use_global_device_ids=true, to_apply=%region_6.7 | all-reduce | flops 16 | bytes 128 | tf_op jit(solution)/shard_map/psum | solution.py:201
  135.0 18.5 %psum.53 = f32[16]{0:T(128)S(1)} all-reduce(f32[16]{0:T(128)S(1)} %psum.52), channel_id=1, replica_groups=mesh['sky'=16,'depth'=8] {'depth'}, use_global_device_ids=true, to_apply=%region_7.8 | all-reduce | flops 16 | bytes 128 | tf_op jit(solution)/shard_map/psum | solution.py:202
  154.8 5.4 %fusion.37 = f32[16,128,128]{2,1,0:T(8,128)S(1)} fusion(f32[16]{0:T(128)S(1)} %get-tuple-element.1089, f32[16]{0:T(128)S(1)} %add_multiply_fusion.4, f32[16,128,128]{2,1,0:T(8,128)S(1)} %get-tuple-element.1163), kind=kLoop, calls=%fused_computation.105 | loop fusion | flops 29097984 | bytes 2097280 | tf_op jit(solution)/shard_map/reduce_sum | solution.py:44
  160.6 14.3 %while.68 = (s32[]{:T(128)}, f32[3,24,128]{2,1,0:T(8,128)S(1)}, f32[3,24,128]{2,1,0:T(8,128)S(1)}, f32[24,128]{1,0:T(8,128)S(1)}, f32[24,128]{1,0:T(8,128)S(1)},...) while((s32[]{:T(128)}, f32[3,24,128]{2,1,0:T(8,128)S(1)}, ...), condition=%wide.region_16.17_spmd.clone, body=%wide.region_11.0_spmd.clone.sunk | while | flops 18740276 | bytes 4916107 | solution.py:89
  161.4 2.7 fusion.94
  166.1 2.7 fusion.94
  170.9 2.7 fusion.94
  179.6 2.4 collective-permute-start.30
  182.0 3.2 collective-permute-start.25
  185.9 4.7 collective-permute-start.31
  194.1 2.5 collective-permute-start.33
  196.6 5.6 %collective-permute-start.32 = (f32[3,3,128]{2,1,0:T(4,128)S(1)}, f32[3,3,128]{2,1,0:T(4,128)S(1)}, u32[]{:S(2)}, u32[]{:S(2)}) collective-permute-start(f32[3,3,128]{2,1,0:T(4,128)S(1)} %collective-permute-done.31), channel_id=1, source_target_pairs={{0,1},{1,2},{2,3},{3,4},{4,5},{5,6},{6,7},{8,9},{9,10},{10,11},{11... | collective-permute-start | bytes 13832 | tf_op jit(solution)/shard_map/ppermute | solution.py:21
  204.2 2.9 collective-permute-done.35
  207.9 62.5 %all-reduce = (f32[]{:T(128)}, f32[]{:T(128)}) all-reduce(f32[]{:T(128)} %get-tuple-element.1159, f32[]{:T(128)} %fusion.76), channel_id=1, replica_groups=mesh['sky'=16,'depth'=8] {'sky','depth'}, use_global_device_ids=true, to_apply=%region_18.19 | all-reduce | flops 2 | bytes 16 | tf_op jit(solution)/shard_map/psum | solution.py:221
  274.4 4.9 %collective-permute-done.36 = f32[3,3,128]{2,1,0:T(4,128)S(1)} collective-permute-done((f32[3,3,128]{2,1,0:T(4,128)S(1)}, f32[3,3,128]{2,1,0:T(4,128)S(1)}, u32[]{:S(2)}, u32[]{:S(2)}) %collective-permute-start.36) | collective-permute-done | bytes 4640 | tf_op jit(solution)/shard_map/ppermute | solution.py:15
  279.4 4.5 collective-permute-start.37
  283.9 5.1 %fusion.42 = f32[16]{0:T(128)S(1)} fusion(f32[16,128,128]{2,1,0:T(8,128)S(1)} %add_sqrt_fusion.4, f32[16,128,128]{2,1,0:T(8,128)S(1)} %get-tuple-element.1164, f32[16]{0:T(128)S(1)} %add_multiply_fusion.4), kind=kLoop, calls=%fused_computation.110 | loop fusion | flops 25165808 | bytes 2097280 | tf_op jit(solution)/shard_map/reduce_sum | solution.py:37
  289.8 1.9 collective-permute-start.41
  291.7 2.4 collective-permute-start.42
  294.2 4.8 collective-permute-start.43
  302.4 2.5 collective-permute-start.45
  304.9 4.7 collective-permute-start.44
  311.7 2.9 collective-permute-done.47
  314.7 10.7 %while.71 = (s32[]{:T(128)}, f32[16]{0:T(128)S(1)}, f32[24,128]{1,0:T(8,128)S(1)}, f32[24,128]{1,0:T(8,128)S(1)}, f32[3,24,128]{2,1,0:T(8,128)S(1)}, /*index=5*/...) while((s32[]{:T(128)}, f32[16]{0:T(128)S(1)}, ...), condition=%wide.region_26.27_spmd.clone, body=%wide.region_23.26_spmd.clone.sunk | while | flops 14286903 | bytes 3244889 | solution.py:71
  315.7 2.5 fusion.100
  319.2 2.5 fusion.100
  322.8 2.5 fusion.100
  325.3 30.2 %psum.56 = f32[16]{0:T(128)S(1)} all-reduce(f32[16]{0:T(128)S(1)} %multiply_add_fusion.1), channel_id=1, replica_groups=mesh['sky'=16,'depth'=8] {'sky'}, use_global_device_ids=true, to_apply=%region_27.28 | all-reduce | flops 16 | bytes 128 | tf_op jit(solution)/shard_map/psum | solution.py:201
  355.5 17.9 %psum.57 = f32[16]{0:T(128)S(1)} all-reduce(f32[16]{0:T(128)S(1)} %psum.56), channel_id=1, replica_groups=mesh['sky'=16,'depth'=8] {'depth'}, use_global_device_ids=true, to_apply=%region_28.29 | all-reduce | flops 16 | bytes 128 | tf_op jit(solution)/shard_map/psum | solution.py:202
  374.6 5.4 %fusion.43 = f32[16,128,128]{2,1,0:T(8,128)S(1)} fusion(f32[16]{0:T(128)S(1)} %get-tuple-element.1087, f32[16,128,128]{2,1,0:T(8,128)S(1)} %add_sqrt_fusion.4, f32[16]{0:T(128)S(1)} %add_multiply_fusion.4), kind=kLoop, calls=%fused_computation.111 | loop fusion | flops 29097984 | bytes 2097280 | tf_op jit(solution)/shard_map/reduce_sum | solution.py:44
  380.4 14.3 %while.69 = (s32[]{:T(128)}, f32[3,24,128]{2,1,0:T(8,128)S(1)}, f32[3,24,128]{2,1,0:T(8,128)S(1)}, f32[24,128]{1,0:T(8,128)S(1)}, f32[24,128]{1,0:T(8,128)S(1)},...) while((s32[]{:T(128)}, f32[3,24,128]{2,1,0:T(8,128)S(1)}, ...), condition=%wide.region_37.38_spmd.clone, body=%wide.region_32.0_spmd.clone.sunk | while | flops 18740276 | bytes 4916107 | solution.py:89
  381.2 2.7 fusion.96
  386.0 2.7 fusion.96
  390.7 2.7 fusion.96
  399.0 2.4 collective-permute-start.54
  401.5 3.2 collective-permute-start.49
  405.4 4.8 collective-permute-start.55
  413.5 2.5 collective-permute-start.57
  416.0 5.5 %collective-permute-start.56 = (f32[3,3,128]{2,1,0:T(4,128)S(1)}, f32[3,3,128]{2,1,0:T(4,128)S(1)}, u32[]{:S(2)}, u32[]{:S(2)}) collective-permute-start(f32[3,3,128]{2,1,0:T(4,128)S(1)} %collective-permute-done.55), channel_id=1, source_target_pairs={{0,1},{1,2},{2,3},{3,4},{4,5},{5,6},{6,7},{8,9},{9,10},{10,11},{11... | collective-permute-start | bytes 13832 | tf_op jit(solution)/shard_map/ppermute | solution.py:21
  423.6 2.9 collective-permute-done.59
  427.3 62.3 %psum.58 = f32[]{:T(128)} all-reduce(f32[]{:T(128)} %get-tuple-element.1161), channel_id=1, replica_groups=mesh['sky'=16,'depth'=8] {'sky','depth'}, use_global_device_ids=true, to_apply=%region_39.40 | all-reduce | flops 1 | bytes 8 | tf_op jit(solution)/shard_map/psum | solution.py:221
  (339 shorter events, 77.3 us)
Async XLA Ops:
  0.0 26.6 %copy-start = (f32[3,16,128]{2,1,0:T(8,128)S(1)}, f32[3,16,128]{2,1,0:T(8,128)}, u32[]{:S(2)}) copy-start(f32[3,16,128]{2,1,0:T(8,128)} %param.15) | copy-start | bytes 73732
  0.0 27.7 %copy-start.3 = (s32[1,128]{1,0:T(1,128)S(1)}, s32[1,128]{1,0:T(1,128)}, u32[]{:S(2)}) copy-start(s32[1,128]{1,0:T(1,128)} %param.18) | copy-start | bytes 1540
  0.0 28.5 %copy-start.5 = (s32[1,128,3]{1,0,2:T(1,128)S(1)}, s32[1,128,3]{1,0,2:T(1,128)}, u32[]{:S(2)}) copy-start(s32[1,128,3]{1,0,2:T(1,128)} %param.20) | copy-start | bytes 4612
  14.3 23.5 %collective-permute-start = (s32[3]{0:T(128)S(1)}, s32[3]{0:T(128)S(1)}, u32[]{:S(2)}, u32[]{:S(2)}) collective-permute-start(s32[3]{0:T(128)S(1)} %get-tuple-element.1142), channel_id=1, source_target_pairs={{0,8},{8,16},{16,24},{24,32},{32,40},{40,48},{48,56},{56,64},{64,7... | collective-permute-start | bytes 44 | tf_op jit(solution)/shard_map/ppermute | solution.py:15
  16.8 22.9 %collective-permute-start.2 = (s32[3]{0:T(128)S(1)}, s32[3]{0:T(128)S(1)}, u32[]{:S(2)}, u32[]{:S(2)}) collective-permute-start(s32[3]{0:T(128)S(1)} %get-tuple-element.1141), channel_id=1, source_target_pairs={{0,8},{8,16},{16,24},{24,32},{32,40},{40,48},{48,56},{56,64},{64,7... | collective-permute-start | bytes 44 | tf_op jit(solution)/shard_map/ppermute | solution.py:15
  18.5 26.1 %collective-permute-start.3 = (s32[3]{0:T(128)S(1)}, s32[3]{0:T(128)S(1)}, u32[]{:S(2)}, u32[]{:S(2)}) collective-permute-start(s32[3]{0:T(128)S(1)} %get-tuple-element.1140), channel_id=1, source_target_pairs={{0,8},{8,16},{16,24},{24,32},{32,40},{40,48},{48,56},{56,64},{64,7... | collective-permute-start | bytes 44 | tf_op jit(solution)/shard_map/ppermute | solution.py:15
  19.8 24.9 %collective-permute-start.5 = (s32[3]{0:T(128)S(1)}, s32[3]{0:T(128)S(1)}, u32[]{:S(2)}, u32[]{:S(2)}) collective-permute-start(s32[3]{0:T(128)S(1)} %get-tuple-element.1139), channel_id=1, source_target_pairs={{0,1},{1,2},{2,3},{3,4},{4,5},{5,6},{6,7},{8,9},{9,10},{10,11},{11... | collective-permute-start | bytes 44 | tf_op jit(solution)/shard_map/ppermute | solution.py:21
  26.5 44.2 %collective-permute-start.12 = (f32[3,3,128]{2,1,0:T(4,128)S(1)}, f32[3,3,128]{2,1,0:T(4,128)S(1)}, u32[]{:S(2)}, u32[]{:S(2)}) collective-permute-start(f32[3,3,128]{2,1,0:T(4,128)S(1)} %get-tuple-element.1133), channel_id=1, source_target_pairs={{0,8},{8,16},{16,24},{24,32},{32,40},{40,48},{48,56},{56,64},{64,7... | collective-permute-start | bytes 13832 | tf_op jit(solution)/shard_map/ppermute | solution.py:15
  37.8 7.0 %collective-permute-start.6 = (s32[3]{0:T(128)S(1)}, s32[3]{0:T(128)S(1)}, u32[]{:S(2)}, u32[]{:S(2)}) collective-permute-start(s32[3]{0:T(128)S(1)} %get-tuple-element.1138), channel_id=1, source_target_pairs={{1,0},{2,1},{3,2},{4,3},{5,4},{6,5},{7,6},{9,8},{10,9},{11,10},{12... | collective-permute-start | bytes 44 | tf_op jit(solution)/shard_map/ppermute | solution.py:21
  39.8 6.4 %collective-permute-start.7 = (s32[3]{0:T(128)S(1)}, s32[3]{0:T(128)S(1)}, u32[]{:S(2)}, u32[]{:S(2)}) collective-permute-start(s32[3]{0:T(128)S(1)} %get-tuple-element.1137), channel_id=1, source_target_pairs={{0,120},{8,0},{16,8},{24,16},{32,24},{40,32},{48,40},{56,48},{64,5... | collective-permute-start | bytes 44 | tf_op jit(solution)/shard_map/ppermute | solution.py:15
  44.6 2.9 collective-permute-start.9
  44.7 7.9 %collective-permute-start.10 = (s32[3]{0:T(128)S(1)}, s32[3]{0:T(128)S(1)}, u32[]{:S(2)}, u32[]{:S(2)}) collective-permute-start(s32[3]{0:T(128)S(1)} %get-tuple-element.1135), channel_id=1, source_target_pairs={{0,120},{8,0},{16,8},{24,16},{32,24},{40,32},{48,40},{56,48},{64,5... | collective-permute-start | bytes 44 | tf_op jit(solution)/shard_map/ppermute | solution.py:15
  44.8 33.7 %collective-permute-start.14 = (f32[3,3,128]{2,1,0:T(4,128)S(1)}, f32[3,3,128]{2,1,0:T(4,128)S(1)}, u32[]{:S(2)}, u32[]{:S(2)}) collective-permute-start(f32[3,3,128]{2,1,0:T(4,128)S(1)} %get-tuple-element.1132), channel_id=1, source_target_pairs={{0,8},{8,16},{16,24},{24,32},{32,40},{40,48},{48,56},{56,64},{64,7... | collective-permute-start | bytes 13832 | tf_op jit(solution)/shard_map/ppermute | solution.py:15
  46.2 33.1 %collective-permute-start.15 = (f32[3,3,128]{2,1,0:T(4,128)S(1)}, f32[3,3,128]{2,1,0:T(4,128)S(1)}, u32[]{:S(2)}, u32[]{:S(2)}) collective-permute-start(f32[3,3,128]{2,1,0:T(4,128)S(1)} %get-tuple-element.1131), channel_id=1, source_target_pairs={{0,8},{8,16},{16,24},{24,32},{32,40},{40,48},{48,56},{56,64},{64,7... | collective-permute-start | bytes 13832 | tf_op jit(solution)/shard_map/ppermute | solution.py:15
  47.5 44.3 %collective-permute-start.17 = (f32[3,3,128]{2,1,0:T(4,128)S(1)}, f32[3,3,128]{2,1,0:T(4,128)S(1)}, u32[]{:S(2)}, u32[]{:S(2)}) collective-permute-start(f32[3,3,128]{2,1,0:T(4,128)S(1)} %get-tuple-element.1130), channel_id=1, source_target_pairs={{0,1},{1,2},{2,3},{3,4},{4,5},{5,6},{6,7},{8,9},{9,10},{10,11},{11... | collective-permute-start | bytes 13832 | tf_op jit(solution)/shard_map/ppermute | solution.py:21
  52.6 3.0 collective-permute-start.1
  55.6 5.0 %collective-permute-start.4 = (s32[3]{0:T(128)S(1)}, s32[3]{0:T(128)S(1)}, u32[]{:S(2)}, u32[]{:S(2)}) collective-permute-start(s32[3]{0:T(128)S(1)} %collective-permute-done.3), channel_id=1, source_target_pairs={{1,0},{2,1},{3,2},{4,3},{5,4},{6,5},{7,6},{9,8},{10,9},{11,10},{12... | collective-permute-start | bytes 44 | tf_op jit(solution)/shard_map/ppermute | solution.py:21
  60.6 3.0 collective-permute-start.8
  63.6 5.0 %collective-permute-start.11 = (s32[3]{0:T(128)S(1)}, s32[3]{0:T(128)S(1)}, u32[]{:S(2)}, u32[]{:S(2)}) collective-permute-start(s32[3]{0:T(128)S(1)} %collective-permute-done.10), channel_id=1, source_target_pairs={{1,0},{2,1},{3,2},{4,3},{5,4},{6,5},{7,6},{9,8},{10,9},{11,10},{12... | collective-permute-start | bytes 44 | tf_op jit(solution)/shard_map/ppermute | solution.py:21
  68.6 23.3 %collective-permute-start.18 = (f32[3,3,128]{2,1,0:T(4,128)S(1)}, f32[3,3,128]{2,1,0:T(4,128)S(1)}, u32[]{:S(2)}, u32[]{:S(2)}) collective-permute-start(f32[3,3,128]{2,1,0:T(4,128)S(1)} %get-tuple-element.1129), channel_id=1, source_target_pairs={{1,0},{2,1},{3,2},{4,3},{5,4},{6,5},{7,6},{9,8},{10,9},{11,10},{12... | collective-permute-start | bytes 13832 | tf_op jit(solution)/shard_map/ppermute | solution.py:21
  70.6 4.4 collective-permute-start.13
  75.0 6.2 %collective-permute-start.19 = (f32[3,3,128]{2,1,0:T(4,128)S(1)}, f32[3,3,128]{2,1,0:T(4,128)S(1)}, u32[]{:S(2)}, u32[]{:S(2)}) collective-permute-start(f32[3,3,128]{2,1,0:T(4,128)S(1)} %get-tuple-element.1128), channel_id=1, source_target_pairs={{0,120},{8,0},{16,8},{24,16},{32,24},{40,32},{48,40},{56,48},{64,5... | collective-permute-start | bytes 13832 | tf_op jit(solution)/shard_map/ppermute | solution.py:15
  78.5 5.8 %collective-permute-start.22 = (f32[3,3,128]{2,1,0:T(4,128)S(1)}, f32[3,3,128]{2,1,0:T(4,128)S(1)}, u32[]{:S(2)}, u32[]{:S(2)}) collective-permute-start(f32[3,3,128]{2,1,0:T(4,128)S(1)} %get-tuple-element.1127), channel_id=1, source_target_pairs={{0,120},{8,0},{16,8},{24,16},{32,24},{40,32},{48,40},{56,48},{64,5... | collective-permute-start | bytes 13832 | tf_op jit(solution)/shard_map/ppermute | solution.py:15
  79.3 10.6 %collective-permute-start.16 = (f32[3,3,128]{2,1,0:T(4,128)S(1)}, f32[3,3,128]{2,1,0:T(4,128)S(1)}, u32[]{:S(2)}, u32[]{:S(2)}) collective-permute-start(f32[3,3,128]{2,1,0:T(4,128)S(1)} %collective-permute-done.15), channel_id=1, source_target_pairs={{1,0},{2,1},{3,2},{4,3},{5,4},{6,5},{7,6},{9,8},{10,9},{11,10},{12... | collective-permute-start | bytes 13832 | tf_op jit(solution)/shard_map/ppermute | solution.py:21
  81.3 10.7 %collective-permute-start.21 = (f32[3,3,128]{2,1,0:T(4,128)S(1)}, f32[3,3,128]{2,1,0:T(4,128)S(1)}, u32[]{:S(2)}, u32[]{:S(2)}) collective-permute-start(f32[3,3,128]{2,1,0:T(4,128)S(1)} %get-tuple-element.1134), channel_id=1, source_target_pairs={{0,120},{8,0},{16,8},{24,16},{32,24},{40,32},{48,40},{56,48},{64,5... | collective-permute-start | bytes 13832 | tf_op jit(solution)/shard_map/ppermute | solution.py:15
  84.3 7.6 %collective-permute-start.20 = (f32[3,3,128]{2,1,0:T(4,128)S(1)}, f32[3,3,128]{2,1,0:T(4,128)S(1)}, u32[]{:S(2)}, u32[]{:S(2)}) collective-permute-start(f32[3,3,128]{2,1,0:T(4,128)S(1)} %collective-permute-done.19), channel_id=1, source_target_pairs={{0,1},{1,2},{2,3},{3,4},{4,5},{5,6},{6,7},{8,9},{9,10},{10,11},{11... | collective-permute-start | bytes 13832 | tf_op jit(solution)/shard_map/ppermute | solution.py:21
  89.9 4.9 %collective-permute-start.23 = (f32[3,3,128]{2,1,0:T(4,128)S(1)}, f32[3,3,128]{2,1,0:T(4,128)S(1)}, u32[]{:S(2)}, u32[]{:S(2)}) collective-permute-start(f32[3,3,128]{2,1,0:T(4,128)S(1)} %collective-permute-done.22), channel_id=1, source_target_pairs={{1,0},{2,1},{3,2},{4,3},{5,4},{6,5},{7,6},{9,8},{10,9},{11,10},{12... | collective-permute-start | bytes 13832 | tf_op jit(solution)/shard_map/ppermute | solution.py:21
  94.9 59.8 %copy-start.4 = (f32[16]{0:T(128)S(1)}, f32[16]{0:T(128)}, u32[]{:S(2)}) copy-start(f32[16]{0:T(128)} %param.17) | copy-start | bytes 196
  174.9 7.1 %collective-permute-start.24 = (f32[3,3,128]{2,1,0:T(4,128)S(1)}, f32[3,3,128]{2,1,0:T(4,128)S(1)}, u32[]{:S(2)}, u32[]{:S(2)}) collective-permute-start(f32[3,3,128]{2,1,0:T(4,128)S(1)} %get-tuple-element.1125), channel_id=1, source_target_pairs={{0,8},{8,16},{16,24},{24,32},{32,40},{40,48},{48,56},{56,64},{64,7... | collective-permute-start | bytes 13832 | tf_op jit(solution)/shard_map/ppermute | solution.py:15
  177.5 13.2 %collective-permute-start.26 = (f32[3,3,128]{2,1,0:T(4,128)S(1)}, f32[3,3,128]{2,1,0:T(4,128)S(1)}, u32[]{:S(2)}, u32[]{:S(2)}) collective-permute-start(f32[3,3,128]{2,1,0:T(4,128)S(1)} %get-tuple-element.1124), channel_id=1, source_target_pairs={{0,8},{8,16},{16,24},{24,32},{32,40},{40,48},{48,56},{56,64},{64,7... | collective-permute-start | bytes 13832 | tf_op jit(solution)/shard_map/ppermute | solution.py:15
  177.6 14.6 %collective-permute-start.27 = (f32[3,3,128]{2,1,0:T(4,128)S(1)}, f32[3,3,128]{2,1,0:T(4,128)S(1)}, u32[]{:S(2)}, u32[]{:S(2)}) collective-permute-start(f32[3,3,128]{2,1,0:T(4,128)S(1)} %get-tuple-element.1123), channel_id=1, source_target_pairs={{0,8},{8,16},{16,24},{24,32},{32,40},{40,48},{48,56},{56,64},{64,7... | collective-permute-start | bytes 13832 | tf_op jit(solution)/shard_map/ppermute | solution.py:15
  177.7 26.4 %collective-permute-start.29 = (f32[3,3,128]{2,1,0:T(4,128)S(1)}, f32[3,3,128]{2,1,0:T(4,128)S(1)}, u32[]{:S(2)}, u32[]{:S(2)}) collective-permute-start(f32[3,3,128]{2,1,0:T(4,128)S(1)} %get-tuple-element.1122), channel_id=1, source_target_pairs={{0,1},{1,2},{2,3},{3,4},{4,5},{5,6},{6,7},{8,9},{9,10},{10,11},{11... | collective-permute-start | bytes 13832 | tf_op jit(solution)/shard_map/ppermute | solution.py:21
  179.6 24.5 %collective-permute-start.30 = (f32[3,3,128]{2,1,0:T(4,128)S(1)}, f32[3,3,128]{2,1,0:T(4,128)S(1)}, u32[]{:S(2)}, u32[]{:S(2)}) collective-permute-start(f32[3,3,128]{2,1,0:T(4,128)S(1)} %get-tuple-element.1121), channel_id=1, source_target_pairs={{1,0},{2,1},{3,2},{4,3},{5,4},{6,5},{7,6},{9,8},{10,9},{11,10},{12... | collective-permute-start | bytes 13832 | tf_op jit(solution)/shard_map/ppermute | solution.py:21
  182.0 3.9 collective-permute-start.25
  185.9 8.1 %collective-permute-start.31 = (f32[3,3,128]{2,1,0:T(4,128)S(1)}, f32[3,3,128]{2,1,0:T(4,128)S(1)}, u32[]{:S(2)}, u32[]{:S(2)}) collective-permute-start(f32[3,3,128]{2,1,0:T(4,128)S(1)} %get-tuple-element.1120), channel_id=1, source_target_pairs={{0,120},{8,0},{16,8},{24,16},{32,24},{40,32},{48,40},{56,48},{64,5... | collective-permute-start | bytes 13832 | tf_op jit(solution)/shard_map/ppermute | solution.py:15
  190.7 5.9 %collective-permute-start.34 = (f32[3,3,128]{2,1,0:T(4,128)S(1)}, f32[3,3,128]{2,1,0:T(4,128)S(1)}, u32[]{:S(2)}, u32[]{:S(2)}) collective-permute-start(f32[3,3,128]{2,1,0:T(4,128)S(1)} %get-tuple-element.1119), channel_id=1, source_target_pairs={{0,120},{8,0},{16,8},{24,16},{32,24},{40,32},{48,40},{56,48},{64,5... | collective-permute-start | bytes 13832 | tf_op jit(solution)/shard_map/ppermute | solution.py:15
  192.2 10.0 %collective-permute-start.28 = (f32[3,3,128]{2,1,0:T(4,128)S(1)}, f32[3,3,128]{2,1,0:T(4,128)S(1)}, u32[]{:S(2)}, u32[]{:S(2)}) collective-permute-start(f32[3,3,128]{2,1,0:T(4,128)S(1)} %collective-permute-done.27), channel_id=1, source_target_pairs={{1,0},{2,1},{3,2},{4,3},{5,4},{6,5},{7,6},{9,8},{10,9},{11,10},{12... | collective-permute-start | bytes 13832 | tf_op jit(solution)/shard_map/ppermute | solution.py:21
  194.1 10.1 %collective-permute-start.33 = (f32[3,3,128]{2,1,0:T(4,128)S(1)}, f32[3,3,128]{2,1,0:T(4,128)S(1)}, u32[]{:S(2)}, u32[]{:S(2)}) collective-permute-start(f32[3,3,128]{2,1,0:T(4,128)S(1)} %get-tuple-element.1126), channel_id=1, source_target_pairs={{0,120},{8,0},{16,8},{24,16},{32,24},{40,32},{48,40},{56,48},{64,5... | collective-permute-start | bytes 13832 | tf_op jit(solution)/shard_map/ppermute | solution.py:15
  196.6 7.6 %collective-permute-start.32 = (f32[3,3,128]{2,1,0:T(4,128)S(1)}, f32[3,3,128]{2,1,0:T(4,128)S(1)}, u32[]{:S(2)}, u32[]{:S(2)}) collective-permute-start(f32[3,3,128]{2,1,0:T(4,128)S(1)} %collective-permute-done.31), channel_id=1, source_target_pairs={{0,1},{1,2},{2,3},{3,4},{4,5},{5,6},{6,7},{8,9},{9,10},{10,11},{11... | collective-permute-start | bytes 13832 | tf_op jit(solution)/shard_map/ppermute | solution.py:21
  202.1 4.9 %collective-permute-start.35 = (f32[3,3,128]{2,1,0:T(4,128)S(1)}, f32[3,3,128]{2,1,0:T(4,128)S(1)}, u32[]{:S(2)}, u32[]{:S(2)}) collective-permute-start(f32[3,3,128]{2,1,0:T(4,128)S(1)} %collective-permute-done.34), channel_id=1, source_target_pairs={{1,0},{2,1},{3,2},{4,3},{5,4},{6,5},{7,6},{9,8},{10,9},{11,10},{12... | collective-permute-start | bytes 13832 | tf_op jit(solution)/shard_map/ppermute | solution.py:21
  273.5 5.9 %collective-permute-start.36 = (f32[3,3,128]{2,1,0:T(4,128)S(1)}, f32[3,3,128]{2,1,0:T(4,128)S(1)}, u32[]{:S(2)}, u32[]{:S(2)}) collective-permute-start(f32[3,3,128]{2,1,0:T(4,128)S(1)} %bitcast.335), channel_id=1, source_target_pairs={{0,8},{8,16},{16,24},{24,32},{32,40},{40,48},{48,56},{56,64},{64,7... | collective-permute-start | bytes 13832 | tf_op jit(solution)/shard_map/ppermute | solution.py:15
  279.4 14.8 %collective-permute-start.37 = (f32[3,3,128]{2,1,0:T(4,128)S(1)}, f32[3,3,128]{2,1,0:T(4,128)S(1)}, u32[]{:S(2)}, u32[]{:S(2)}) collective-permute-start(f32[3,3,128]{2,1,0:T(4,128)S(1)} %collective-permute-done.36), channel_id=1, source_target_pairs={{0,1},{1,2},{2,3},{3,4},{4,5},{5,6},{6,7},{8,9},{9,10},{10,11},{11... | collective-permute-start | bytes 13832 | tf_op jit(solution)/shard_map/ppermute | solution.py:21
  289.6 9.4 %collective-permute-start.38 = (f32[3,3,128]{2,1,0:T(4,128)S(1)}, f32[3,3,128]{2,1,0:T(4,128)S(1)}, u32[]{:S(2)}, u32[]{:S(2)}) collective-permute-start(f32[3,3,128]{2,1,0:T(4,128)S(1)} %bitcast.332), channel_id=1, source_target_pairs={{0,8},{8,16},{16,24},{24,32},{32,40},{40,48},{48,56},{56,64},{64,7... | collective-permute-start | bytes 13832 | tf_op jit(solution)/shard_map/ppermute | solution.py:15
  289.7 10.8 %collective-permute-start.39 = (f32[3,3,128]{2,1,0:T(4,128)S(1)}, f32[3,3,128]{2,1,0:T(4,128)S(1)}, u32[]{:S(2)}, u32[]{:S(2)}) collective-permute-start(f32[3,3,128]{2,1,0:T(4,128)S(1)} %bitcast.331), channel_id=1, source_target_pairs={{0,8},{8,16},{16,24},{24,32},{32,40},{40,48},{48,56},{56,64},{64,7... | collective-permute-start | bytes 13832 | tf_op jit(solution)/shard_map/ppermute | solution.py:15
  289.8 21.8 %collective-permute-start.41 = (f32[3,3,128]{2,1,0:T(4,128)S(1)}, f32[3,3,128]{2,1,0:T(4,128)S(1)}, u32[]{:S(2)}, u32[]{:S(2)}) collective-permute-start(f32[3,3,128]{2,1,0:T(4,128)S(1)} %bitcast.330), channel_id=1, source_target_pairs={{0,1},{1,2},{2,3},{3,4},{4,5},{5,6},{6,7},{8,9},{9,10},{10,11},{11... | collective-permute-start | bytes 13832 | tf_op jit(solution)/shard_map/ppermute | solution.py:21
  291.7 19.9 %collective-permute-start.42 = (f32[3,3,128]{2,1,0:T(4,128)S(1)}, f32[3,3,128]{2,1,0:T(4,128)S(1)}, u32[]{:S(2)}, u32[]{:S(2)}) collective-permute-start(f32[3,3,128]{2,1,0:T(4,128)S(1)} %bitcast.329), channel_id=1, source_target_pairs={{1,0},{2,1},{3,2},{4,3},{5,4},{6,5},{7,6},{9,8},{10,9},{11,10},{12... | collective-permute-start | bytes 13832 | tf_op jit(solution)/shard_map/ppermute | solution.py:21
  294.2 8.2 %collective-permute-start.43 = (f32[3,3,128]{2,1,0:T(4,128)S(1)}, f32[3,3,128]{2,1,0:T(4,128)S(1)}, u32[]{:S(2)}, u32[]{:S(2)}) collective-permute-start(f32[3,3,128]{2,1,0:T(4,128)S(1)} %bitcast.334), channel_id=1, source_target_pairs={{0,120},{8,0},{16,8},{24,16},{32,24},{40,32},{48,40},{56,48},{64,5... | collective-permute-start | bytes 13832 | tf_op jit(solution)/shard_map/ppermute | solution.py:15
  299.0 5.9 %collective-permute-start.46 = (f32[3,3,128]{2,1,0:T(4,128)S(1)}, f32[3,3,128]{2,1,0:T(4,128)S(1)}, u32[]{:S(2)}, u32[]{:S(2)}) collective-permute-start(f32[3,3,128]{2,1,0:T(4,128)S(1)} %bitcast.333), channel_id=1, source_target_pairs={{0,120},{8,0},{16,8},{24,16},{32,24},{40,32},{48,40},{56,48},{64,5... | collective-permute-start | bytes 13832 | tf_op jit(solution)/shard_map/ppermute | solution.py:15
  300.4 9.2 %collective-permute-start.40 = (f32[3,3,128]{2,1,0:T(4,128)S(1)}, f32[3,3,128]{2,1,0:T(4,128)S(1)}, u32[]{:S(2)}, u32[]{:S(2)}) collective-permute-start(f32[3,3,128]{2,1,0:T(4,128)S(1)} %collective-permute-done.39), channel_id=1, source_target_pairs={{1,0},{2,1},{3,2},{4,3},{5,4},{6,5},{7,6},{9,8},{10,9},{11,10},{12... | collective-permute-start | bytes 13832 | tf_op jit(solution)/shard_map/ppermute | solution.py:21
  302.4 9.3 %collective-permute-start.45 = (f32[3,3,128]{2,1,0:T(4,128)S(1)}, f32[3,3,128]{2,1,0:T(4,128)S(1)}, u32[]{:S(2)}, u32[]{:S(2)}) collective-permute-start(f32[3,3,128]{2,1,0:T(4,128)S(1)} %bitcast.328), channel_id=1, source_target_pairs={{0,120},{8,0},{16,8},{24,16},{32,24},{40,32},{48,40},{56,48},{64,5... | collective-permute-start | bytes 13832 | tf_op jit(solution)/shard_map/ppermute | solution.py:15
  304.9 6.7 %collective-permute-start.44 = (f32[3,3,128]{2,1,0:T(4,128)S(1)}, f32[3,3,128]{2,1,0:T(4,128)S(1)}, u32[]{:S(2)}, u32[]{:S(2)}) collective-permute-start(f32[3,3,128]{2,1,0:T(4,128)S(1)} %collective-permute-done.43), channel_id=1, source_target_pairs={{0,1},{1,2},{2,3},{3,4},{4,5},{5,6},{6,7},{8,9},{9,10},{10,11},{11... | collective-permute-start | bytes 13832 | tf_op jit(solution)/shard_map/ppermute | solution.py:21
  309.7 4.9 %collective-permute-start.47 = (f32[3,3,128]{2,1,0:T(4,128)S(1)}, f32[3,3,128]{2,1,0:T(4,128)S(1)}, u32[]{:S(2)}, u32[]{:S(2)}) collective-permute-start(f32[3,3,128]{2,1,0:T(4,128)S(1)} %collective-permute-done.46), channel_id=1, source_target_pairs={{1,0},{2,1},{3,2},{4,3},{5,4},{6,5},{7,6},{9,8},{10,9},{11,10},{12... | collective-permute-start | bytes 13832 | tf_op jit(solution)/shard_map/ppermute | solution.py:21
  394.7 6.7 %collective-permute-start.48 = (f32[3,3,128]{2,1,0:T(4,128)S(1)}, f32[3,3,128]{2,1,0:T(4,128)S(1)}, u32[]{:S(2)}, u32[]{:S(2)}) collective-permute-start(f32[3,3,128]{2,1,0:T(4,128)S(1)} %get-tuple-element.1109), channel_id=1, source_target_pairs={{0,8},{8,16},{16,24},{24,32},{32,40},{40,48},{48,56},{56,64},{64,7... | collective-permute-start | bytes 13832 | tf_op jit(solution)/shard_map/ppermute | solution.py:15
  396.9 13.2 %collective-permute-start.50 = (f32[3,3,128]{2,1,0:T(4,128)S(1)}, f32[3,3,128]{2,1,0:T(4,128)S(1)}, u32[]{:S(2)}, u32[]{:S(2)}) collective-permute-start(f32[3,3,128]{2,1,0:T(4,128)S(1)} %get-tuple-element.1108), channel_id=1, source_target_pairs={{0,8},{8,16},{16,24},{24,32},{32,40},{40,48},{48,56},{56,64},{64,7... | collective-permute-start | bytes 13832 | tf_op jit(solution)/shard_map/ppermute | solution.py:15
  397.0 14.6 %collective-permute-start.51 = (f32[3,3,128]{2,1,0:T(4,128)S(1)}, f32[3,3,128]{2,1,0:T(4,128)S(1)}, u32[]{:S(2)}, u32[]{:S(2)}) collective-permute-start(f32[3,3,128]{2,1,0:T(4,128)S(1)} %get-tuple-element.1107), channel_id=1, source_target_pairs={{0,8},{8,16},{16,24},{24,32},{32,40},{40,48},{48,56},{56,64},{64,7... | collective-permute-start | bytes 13832 | tf_op jit(solution)/shard_map/ppermute | solution.py:15
  397.1 26.4 %collective-permute-start.53 = (f32[3,3,128]{2,1,0:T(4,128)S(1)}, f32[3,3,128]{2,1,0:T(4,128)S(1)}, u32[]{:S(2)}, u32[]{:S(2)}) collective-permute-start(f32[3,3,128]{2,1,0:T(4,128)S(1)} %get-tuple-element.1106), channel_id=1, source_target_pairs={{0,1},{1,2},{2,3},{3,4},{4,5},{5,6},{6,7},{8,9},{9,10},{10,11},{11... | collective-permute-start | bytes 13832 | tf_op jit(solution)/shard_map/ppermute | solution.py:21
  399.0 24.5 %collective-permute-start.54 = (f32[3,3,128]{2,1,0:T(4,128)S(1)}, f32[3,3,128]{2,1,0:T(4,128)S(1)}, u32[]{:S(2)}, u32[]{:S(2)}) collective-permute-start(f32[3,3,128]{2,1,0:T(4,128)S(1)} %get-tuple-element.1105), channel_id=1, source_target_pairs={{1,0},{2,1},{3,2},{4,3},{5,4},{6,5},{7,6},{9,8},{10,9},{11,10},{12... | collective-permute-start | bytes 13832 | tf_op jit(solution)/shard_map/ppermute | solution.py:21
  401.5 3.9 collective-permute-start.49
  405.4 8.1 %collective-permute-start.55 = (f32[3,3,128]{2,1,0:T(4,128)S(1)}, f32[3,3,128]{2,1,0:T(4,128)S(1)}, u32[]{:S(2)}, u32[]{:S(2)}) collective-permute-start(f32[3,3,128]{2,1,0:T(4,128)S(1)} %get-tuple-element.1104), channel_id=1, source_target_pairs={{0,120},{8,0},{16,8},{24,16},{32,24},{40,32},{48,40},{56,48},{64,5... | collective-permute-start | bytes 13832 | tf_op jit(solution)/shard_map/ppermute | solution.py:15
  410.1 5.9 %collective-permute-start.58 = (f32[3,3,128]{2,1,0:T(4,128)S(1)}, f32[3,3,128]{2,1,0:T(4,128)S(1)}, u32[]{:S(2)}, u32[]{:S(2)}) collective-permute-start(f32[3,3,128]{2,1,0:T(4,128)S(1)} %get-tuple-element.1103), channel_id=1, source_target_pairs={{0,120},{8,0},{16,8},{24,16},{32,24},{40,32},{48,40},{56,48},{64,5... | collective-permute-start | bytes 13832 | tf_op jit(solution)/shard_map/ppermute | solution.py:15
  411.6 10.0 %collective-permute-start.52 = (f32[3,3,128]{2,1,0:T(4,128)S(1)}, f32[3,3,128]{2,1,0:T(4,128)S(1)}, u32[]{:S(2)}, u32[]{:S(2)}) collective-permute-start(f32[3,3,128]{2,1,0:T(4,128)S(1)} %collective-permute-done.51), channel_id=1, source_target_pairs={{1,0},{2,1},{3,2},{4,3},{5,4},{6,5},{7,6},{9,8},{10,9},{11,10},{12... | collective-permute-start | bytes 13832 | tf_op jit(solution)/shard_map/ppermute | solution.py:21
  413.5 10.1 %collective-permute-start.57 = (f32[3,3,128]{2,1,0:T(4,128)S(1)}, f32[3,3,128]{2,1,0:T(4,128)S(1)}, u32[]{:S(2)}, u32[]{:S(2)}) collective-permute-start(f32[3,3,128]{2,1,0:T(4,128)S(1)} %get-tuple-element.1110), channel_id=1, source_target_pairs={{0,120},{8,0},{16,8},{24,16},{32,24},{40,32},{48,40},{56,48},{64,5... | collective-permute-start | bytes 13832 | tf_op jit(solution)/shard_map/ppermute | solution.py:15
  416.0 7.6 %collective-permute-start.56 = (f32[3,3,128]{2,1,0:T(4,128)S(1)}, f32[3,3,128]{2,1,0:T(4,128)S(1)}, u32[]{:S(2)}, u32[]{:S(2)}) collective-permute-start(f32[3,3,128]{2,1,0:T(4,128)S(1)} %collective-permute-done.55), channel_id=1, source_target_pairs={{0,1},{1,2},{2,3},{3,4},{4,5},{5,6},{6,7},{8,9},{9,10},{10,11},{11... | collective-permute-start | bytes 13832 | tf_op jit(solution)/shard_map/ppermute | solution.py:21
  421.6 4.9 %collective-permute-start.59 = (f32[3,3,128]{2,1,0:T(4,128)S(1)}, f32[3,3,128]{2,1,0:T(4,128)S(1)}, u32[]{:S(2)}, u32[]{:S(2)}) collective-permute-start(f32[3,3,128]{2,1,0:T(4,128)S(1)} %collective-permute-done.58), channel_id=1, source_target_pairs={{1,0},{2,1},{3,2},{4,3},{5,4},{6,5},{7,6},{9,8},{10,9},{11,10},{12... | collective-permute-start | bytes 13832 | tf_op jit(solution)/shard_map/ppermute | solution.py:21
  (2 other events, 53.0 us)
